TPU v7x, 32 devices: a whole 2x2x4 slice. The times are simulated.
32 devices in a mesh: row: 4 (over y, x), col: 8 (over z, core).
Axes of the slice: x: 2, y: 2, z: 4, core: 2. Of those that a mesh axis runs over, the one named last changes fastest.
Arguments:
- throat_owner: int32 [16384, 1], P(('row', 'col')), may hold values from 0 to 3; in each aligned block of 512 rows (0 to 511, 512 to 1023, ...) at most 128 rows name the same one
- throat_interior: int32 [16384], P(('row', 'col')), may hold values from 0 to 895
- throat_offset: int32 [16384], P(('row', 'col')), may hold values from 0 to 4095
- throat_conductance: float32 [16384], P(('row', 'col')), may hold values from 0.1 to 1
- child_update: bfloat16 [7168, 16384], P('col', 'row'), may hold values from -0.09375 to 0.09375
- panel_pores: int32 [4096], replicated, may hold values from 0 to 16383, as said below
- interior_inverse: bfloat16 [7168, 896], P('col'), as said below
- separator_rows: float32 [4096, 16384], P('col', 'row'), may hold values from -6 to 6
Outputs:
- schur_rows: float32 [4096, 16384], P('col', 'row')
Inputs may be any that keep to these rules, and one draw needn't show every extreme that they name: `throat_owner`: in each device's block of 512 throats no owner is named more than 128 times, a bound that some block reaches. `panel_pores`: the 4096 pores are distinct; at most 1536 of them lie in any one owner's range of 4096 pores, and one owner holds exactly 1536. `interior_inverse`: each group's block of 896 rows is lower triangular with diagonal entries between 0.8 and 1.2.
All inputs are finite; a program needn't handle non-finite values.
Results may differ from a plain program's by a relative error of at most 0.01.
Values may be sent and summed in bfloat16 or wider, within the bound.
No kernel may reach another device: no remote copies, remote signals or barrier semaphores. Data moves between devices by JAX's collectives and lax.ppermute only.
A program may use at most 128 MiB of HBM per device.

v0:
```python
import jax
import jax.numpy as jnp
from jax import lax
from jax.sharding import PartitionSpec as P

STEPS = (3, 3, 4, 4, 4, 4, 4, 3, 2, 1)
LATER = 3
STAYS = 1
ALONE = 2


def route_throats(owners, interior, offset, conductance, row_count, owner_width):
    throats = interior.shape[0]
    slot_limit = throats // 4
    order = jnp.arange(throats, dtype=jnp.int32)
    earlier = (owners[None, :] == owners[:, None]) & (order[None, :] < order[:, None])
    rank = jnp.sum(earlier.astype(jnp.int32), axis=1)
    slot = owners * slot_limit + rank
    code = (interior * owner_width + offset + 1).astype(jnp.float32)
    slots = jnp.arange(row_count * slot_limit, dtype=jnp.int32)
    placed = slots[:, None] == slot[None, :]
    codes = jnp.sum(jnp.where(placed, code[None, :], 0.0), axis=1)
    values = jnp.sum(jnp.where(placed, conductance[None, :], 0.0), axis=1)
    block = jnp.stack(
        [codes.reshape(row_count, slot_limit), values.reshape(row_count, slot_limit)], axis=1
    )
    back = lax.all_to_all(block, "row", split_axis=0, concat_axis=0, tiled=True)
    codes = back[:, 0, :].reshape(-1).astype(jnp.int32) - 1
    values = back[:, 1, :].reshape(-1)
    return codes // owner_width, codes % owner_width, values


def add_throats(child_update, pivots, pores, values):
    high = lax.reduce_precision(values, 8, 7)
    low = values - high
    values = jnp.concatenate([high, low]).astype(jnp.bfloat16)
    pivots = jnp.concatenate([pivots, pivots])
    pores = jnp.concatenate([pores, pores])
    rows = jnp.arange(child_update.shape[0], dtype=jnp.int32)
    columns = jnp.arange(child_update.shape[1], dtype=jnp.int32)
    left = jnp.where(rows[:, None] == pivots[None, :], values[None, :], jnp.bfloat16(0))
    right = (pores[:, None] == columns[None, :]).astype(jnp.bfloat16)
    summed = jnp.dot(left, right, preferred_element_type=jnp.float32)
    return (child_update.astype(jnp.float32) + summed).astype(jnp.bfloat16)


def per_device(
    throat_owner,
    throat_interior,
    throat_offset,
    throat_conductance,
    child_update,
    panel_pores,
    interior_inverse,
    separator_rows,
):
    row_count = lax.axis_size("row")
    col_count = lax.axis_size("col")
    row_index = lax.axis_index("row")
    col_index = lax.axis_index("col")
    own_rows, owner_width = separator_rows.shape
    chips = col_count // 2
    core = col_index % 2
    chip = col_index // 2
    square = row_count == 4
    line = chips == 4
    at_end = (chip == 0) | (chip == chips - 1)

    pivots, pores, values = route_throats(
        throat_owner[:, 0],
        throat_interior,
        throat_offset,
        throat_conductance,
        row_count,
        owner_width,
    )
    coupling = add_throats(child_update, pivots, pores, values)
    solved = jnp.dot(interior_inverse, coupling, preferred_element_type=jnp.float32).astype(
        jnp.bfloat16
    )

    local_pores = (panel_pores - row_index * owner_width).reshape(chips, 2, own_rows)
    if line:
        order = jnp.array([[0, 1, 2, 3], [1, 2, 3, 0], [2, 1, 0, 3], [3, 2, 1, 0]], jnp.int32)
        local_pores = jnp.take(local_pores, order[chip], axis=0)
    other_pores = jnp.where(core == 0, local_pores[:, 1], local_pores[:, 0])
    mine_pores = jnp.where(core == 0, local_pores[:, 0], local_pores[:, 1])
    columns = jnp.arange(owner_width, dtype=jnp.int32)

    swap = [(i, i ^ 1) for i in range(col_count)]
    along_x = [(i, i ^ 1) for i in range(row_count)]
    along_y = [(i, i ^ 2) for i in range(row_count)]
    ends = [(i, i ^ 2) for i in range(col_count)]
    inward = [(2 * g + c, 2 * t + c) for g, t in ((0, 1), (3, 2)) for c in range(2)]
    outward = [(2 * g + c, 2 * t + c) for g, t in ((1, 0), (2, 3)) for c in range(2)]
    across = [(2 * g + c, 2 * t + c) for g, t in ((1, 2), (2, 1)) for c in range(2)]

    sizes = [own_rows * s // sum(STEPS) for s in STEPS]
    starts = [sum(sizes[:i]) for i in range(len(sizes))]
    count = len(sizes)
    state = [dict() for _ in sizes]

    def pick(k):
        part = slice(starts[k], starts[k] + sizes[k])
        pores = jnp.concatenate([other_pores[:, part].reshape(-1), mine_pores[:, part].reshape(-1)])
        onehot = (pores[:, None] == columns[None, :]).astype(jnp.bfloat16)
        state[k]["rows"] = lax.dot_general(
            onehot, shared["solved"], (((1,), (1,)), ((), ())), preferred_element_type=jnp.float32
        ).astype(jnp.bfloat16)

    def share(k):
        s = state[k]
        if square:
            s["rows_in"] = lax.ppermute(s["rows"], "row", along_x)
        else:
            s["rows"] = lax.psum(s["rows"], "row")

    def share_again(k):
        s = state[k]
        if square:
            s["rows"] += s.pop("rows_in")
            s["rows_in"] = lax.ppermute(s["rows"], "row", along_y)

    def multiply(k):
        s = state[k]
        rows = s.pop("rows")
        if square:
            rows += s.pop("rows_in")
        half = chips * sizes[k]
        sent, mine = (
            jnp.dot(picked, shared["solved"], preferred_element_type=jnp.float32).astype(jnp.bfloat16)
            for picked in (rows[:half], rows[half:])
        )
        n = sizes[k]
        come = lax.ppermute(sent, "col", swap)
        s["own"] = mine[:n] + come[:n]
        s["rest"] = mine[n:] + come[n:]

    def rides(k):
        return k + LATER < count - ALONE

    def leaving(k):
        s, n = state[k], sizes[k]
        return s.pop("rest")[2 * n :] + s["from_middle"][n:]

    def move_in(k):
        s = state[k]
        if line:
            sent = s["rest"]
            if k >= LATER and rides(k - LATER):
                out = leaving(k - LATER)
                n = out.shape[0]
                sent = jnp.concatenate([jnp.where(at_end, sent[:n], out), sent[n:]], axis=0)
            come = lax.ppermute(sent, "col", ends if k < count - ALONE else inward)
            if k < STAYS:
                s["from_end"] = come
            else:
                flying[k] = come

    def land(k):
        s = state[k]
        if k in flying:
            s["from_end"] = flying.pop(k)

    def move_across(k):
        s = state[k]
        if line:
            n = sizes[k]
            s["from_middle"] = lax.ppermute(s["rest"][: 2 * n] + s["from_end"][n:], "col", across)

    def move_out(k):
        s = state[k]
        if line and not rides(k):
            s["from_inner"] = lax.ppermute(leaving(k), "col", outward)

    def settle(k):
        s = state[k]
        n = sizes[k]
        own = s.pop("own")
        if line:
            here = s["from_end"][:n].astype(jnp.float32) + s["from_middle"][:n].astype(jnp.float32)
            there = state[k + LATER]["from_end"][:n] if rides(k) else s["from_inner"]
            update = own.astype(jnp.float32) + jnp.where(at_end, there.astype(jnp.float32), here)
        else:
            groups = [[2 * g + c for g in range(chips)] for c in range(2)]
            pair = jnp.concatenate([own, s["rest"]], axis=0)
            update = lax.psum_scatter(
                pair, "col", scatter_dimension=0, axis_index_groups=groups, tiled=True
            ).astype(jnp.float32)
        rows = lax.slice_in_dim(shared["out"], starts[k], starts[k] + n, axis=0)
        shared["out"] = lax.dynamic_update_slice(shared["out"], rows - update, (starts[k], 0))

    plan = {}

    def at(turn, stage, *args):
        plan.setdefault(turn, []).append((stage, args))

    for k in reversed(range(count)):
        at(k, pick, k)
        at(k + 1, share, k)
        at(k + 2, share_again, k)
        at(k + 6, land, k)
    for k in reversed(range(count)):
        at(k + 3, multiply, k)
        at(k + 6, move_across, k)
        at(k + 4, move_in, k)
        if not rides(k):
            at(k + 7, move_out, k)
        at(k + (9 if rides(k) else 8), settle, k)
    shared = {"solved": solved, "out": separator_rows}
    flying = {}
    for turn in range(max(plan) + 1):
        shared, state = lax.optimization_barrier((shared, state))
        for stage, args in plan.get(turn, ()):
            stage(*args)
    return shared["out"]


def solution(mesh):
    in_specs = (
        P(("row", "col"), None),
        P(("row", "col")),
        P(("row", "col")),
        P(("row", "col")),
        P("col", "row"),
        P(),
        P("col", None),
        P("col", "row"),
    )
    out_specs = P("col", "row")
    return jax.shard_map(
        per_device, mesh=mesh, in_specs=in_specs, out_specs=out_specs, check_vma=False
    )
```

profile of v0, /device:TPU:0, one launch (start us, length us, event | category | flops | bytes accessed | tf_op | source)
XLA Modules:
  0.0 438.3 jit_solution(14353148838597912746)
XLA Ops:
  2.1 5.2 %all-to-all-start = ((f32[4,2,128]{2,1,0:T(2,128)}), f32[4,2,128]{2,1,0:T(2,128)S(1)}, u32[]{:S(2)}, u32[]{:S(2)}) async-start(f32[4,2,128]{2,1,0:T(2,128)} %pad_maximum_fusion.5), calls=%async_computation | async-start | bytes 8192 | tf_op jit(solution)/shard_map/all_to_all | solution.py:27
  12.0 13.9 %add_convert_fusion.7 = bf16[896,4096]{1,0:T(8,128)(2,1)S(1)} fusion(bf16[896,4096]{1,0:T(8,128)(2,1)} %param.13, s32[1024]{0:T(1024)S(1)} %pad_add_fusion.1, s32[1024]{0:T(1024)S(1)} %pad_add_fusion, bf16[1024]{0:T(1024)(128)(2,1)S(1)} %pad_maximum_fusion.6), kind=kOutput, calls=%fused_computation.3.clone.clone.clone.clone.1 | convolution fusion | flops 7533232128 | bytes 14690304 | tf_op jit(solution)/shard_map/dot_general | solution.py:43
  25.9 9.1 %convert_bitcast_fusion = bf16[896,4096]{0,1:T(8,128)(2,1)S(1)} fusion(bf16[896,896]{1,0:T(8,128)(2,1)S(1)} %copy-done, bf16[896,4096]{1,0:T(8,128)(2,1)S(1)} %add_convert_fusion.7), kind=kOutput, calls=%fused_computation.16 | convolution fusion | flops 6580338688 | bytes 16285696 | tf_op jit(solution)/shard_map/dot_general | solution.py:78
  35.0 3.5 fusion.34
  39.1 3.5 fusion.33
  42.6 11.7 %collective-permute-done = bf16[384,896]{1,0:T(8,128)(2,1)S(1)} collective-permute-done((bf16[384,896]{1,0:T(8,128)(2,1)S(1)}, bf16[384,896]{1,0:T(8,128)(2,1)S(1)}, u32[]{:S(2)}, u32[]{:S(2)}) %collective-permute-start) | collective-permute-done | bytes 688160 | tf_op jit(solution)/shard_map/ppermute | solution.py:114
  57.4 4.5 %fusion.31 = bf16[512,896]{1,0:T(8,128)(2,1)S(1)} fusion(bf16[896,4096]{0,1:T(8,128)(2,1)S(1)} %convert_bitcast_fusion, s32[512]{0:T(512)S(1)} %pad_add_fusion.4), kind=kOutput, calls=%fused_computation.72 | convolution fusion | flops 3760652288 | bytes 8259584 | tf_op jit(solution)/shard_map/dot_general | solution.py:107
  62.0 7.9 %collective-permute-done.1 = bf16[384,896]{1,0:T(8,128)(2,1)S(1)} collective-permute-done((bf16[384,896]{1,0:T(8,128)(2,1)S(1)}, bf16[384,896]{1,0:T(8,128)(2,1)S(1)}, u32[]{:S(2)}, u32[]{:S(2)}) %collective-permute-start.1) | collective-permute-done | bytes 688160 | tf_op jit(solution)/shard_map/ppermute | solution.py:122
  71.5 2.6 convolution_convert_fusion.14
  76.7 2.6 convolution_convert_fusion.15
  79.3 4.5 %fusion.30 = bf16[512,896]{1,0:T(8,128)(2,1)S(1)} fusion(bf16[896,4096]{0,1:T(8,128)(2,1)S(1)} %convert_bitcast_fusion, s32[512]{0:T(512)S(1)} %pad_add_fusion.5), kind=kOutput, calls=%fused_computation.71 | convolution fusion | flops 3760652288 | bytes 8259584 | tf_op jit(solution)/shard_map/dot_general | solution.py:107
  84.0 8.5 %collective-permute-done.4 = bf16[384,896]{1,0:T(8,128)(2,1)S(1)} collective-permute-done((bf16[384,896]{1,0:T(8,128)(2,1)S(1)}, bf16[384,896]{1,0:T(8,128)(2,1)S(1)}, u32[]{:S(2)}, u32[]{:S(2)}) %collective-permute-start.4) | collective-permute-done | bytes 688160 | tf_op jit(solution)/shard_map/ppermute | solution.py:122
  92.5 5.0 %collective-permute-done.5 = bf16[512,896]{1,0:T(8,128)(2,1)S(1)} collective-permute-done((bf16[512,896]{1,0:T(8,128)(2,1)S(1)}, bf16[512,896]{1,0:T(8,128)(2,1)S(1)}, u32[]{:S(2)}, u32[]{:S(2)}) %collective-permute-start.5) | collective-permute-done | bytes 917536 | tf_op jit(solution)/shard_map/ppermute | solution.py:114
  97.6 2.6 convolution_convert_fusion.12
  105.4 2.6 convolution_convert_fusion.13
  108.0 5.0 %fusion.29 = bf16[512,896]{1,0:T(8,128)(2,1)S(1)} fusion(bf16[896,4096]{0,1:T(8,128)(2,1)S(1)} %convert_bitcast_fusion, s32[512]{0:T(512)S(1)} %pad_add_fusion.6), kind=kOutput, calls=%fused_computation.70 | convolution fusion | flops 3760652288 | bytes 8259584 | tf_op jit(solution)/shard_map/dot_general | solution.py:107
  114.0 10.7 %collective-permute-done.8 = bf16[512,896]{1,0:T(8,128)(2,1)S(1)} collective-permute-done((bf16[512,896]{1,0:T(8,128)(2,1)S(1)}, bf16[512,896]{1,0:T(8,128)(2,1)S(1)}, u32[]{:S(2)}, u32[]{:S(2)}) %collective-permute-start.8) | collective-permute-done | bytes 917536 | tf_op jit(solution)/shard_map/ppermute | solution.py:122
  126.1 2.6 collective-permute-done.6
  128.9 3.7 convolution_convert_fusion.8
  137.8 2.4 convolution_convert_fusion.9
  140.2 4.5 %fusion.28 = bf16[512,896]{1,0:T(8,128)(2,1)S(1)} fusion(bf16[896,4096]{0,1:T(8,128)(2,1)S(1)} %convert_bitcast_fusion, s32[512]{0:T(512)S(1)} %pad_add_fusion.7), kind=kOutput, calls=%fused_computation.69 | convolution fusion | flops 3760652288 | bytes 8259584 | tf_op jit(solution)/shard_map/dot_general | solution.py:107
  145.8 10.1 %collective-permute-done.11 = bf16[512,896]{1,0:T(8,128)(2,1)S(1)} collective-permute-done((bf16[512,896]{1,0:T(8,128)(2,1)S(1)}, bf16[512,896]{1,0:T(8,128)(2,1)S(1)}, u32[]{:S(2)}, u32[]{:S(2)}) %collective-permute-start.11) | collective-permute-done | bytes 917536 | tf_op jit(solution)/shard_map/ppermute | solution.py:122
  157.5 3.9 convolution_convert_fusion.6
  164.5 2.4 convolution_convert_fusion.7
  166.8 4.5 %fusion.27 = bf16[512,896]{1,0:T(8,128)(2,1)S(1)} fusion(bf16[896,4096]{0,1:T(8,128)(2,1)S(1)} %convert_bitcast_fusion, s32[512]{0:T(512)S(1)} %pad_add_fusion.8), kind=kOutput, calls=%fused_computation.68 | convolution fusion | flops 3760652288 | bytes 8259584 | tf_op jit(solution)/shard_map/dot_general | solution.py:107
  171.4 4.4 %collective-permute-start.22 = (bf16[192,4096]{1,0:T(8,128)(2,1)S(1)}, bf16[192,4096]{1,0:T(8,128)(2,1)S(1)}, u32[]{:S(2)}, u32[]{:S(2)}) collective-permute-start(bf16[192,4096]{1,0:T(8,128)(2,1)S(1)} %slice_add_fusion.4), channel_id=1, source_target_pairs={{0,2},{1,3},{2,0},{3,1},{4,6},{5,7},{6,4},{7,5},{8,10},{9,11},{10,... | collective-permute-start | bytes 4718600 | tf_op jit(solution)/shard_map/ppermute | solution.py:154
  176.1 9.1 %collective-permute-done.15 = bf16[512,896]{1,0:T(8,128)(2,1)S(1)} collective-permute-done((bf16[512,896]{1,0:T(8,128)(2,1)S(1)}, bf16[512,896]{1,0:T(8,128)(2,1)S(1)}, u32[]{:S(2)}, u32[]{:S(2)}) %collective-permute-start.15) | collective-permute-done | bytes 917536 | tf_op jit(solution)/shard_map/ppermute | solution.py:122
  186.4 1.7 collective-permute-start.18
  188.4 3.7 convolution_convert_fusion.4
  197.1 2.4 convolution_convert_fusion.5
  199.5 4.3 fusion.32
  203.8 4.9 %collective-permute-start.27 = (bf16[192,4096]{1,0:T(8,128)(2,1)}, bf16[192,4096]{1,0:T(8,128)(2,1)S(1)}, u32[]{:S(2)}, u32[]{:S(2)}) collective-permute-start(bf16[192,4096]{1,0:T(8,128)(2,1)} %pad_maximum_fusion), channel_id=1, source_target_pairs={{0,2},{1,3},{2,0},{3,1},{4,6},{5,7},{6,4},{7,5},{8,10},{9,11},{10,... | collective-permute-start | bytes 4718600 | tf_op jit(solution)/shard_map/ppermute | solution.py:154
  209.7 5.4 %collective-permute-done.20 = bf16[512,896]{1,0:T(8,128)(2,1)S(1)} collective-permute-done((bf16[512,896]{1,0:T(8,128)(2,1)S(1)}, bf16[512,896]{1,0:T(8,128)(2,1)S(1)}, u32[]{:S(2)}, u32[]{:S(2)}) %collective-permute-start.20) | collective-permute-done | bytes 917536 | tf_op jit(solution)/shard_map/ppermute | solution.py:122
  218.8 3.7 convolution_convert_fusion.2
  227.4 2.4 convolution_convert_fusion.3
  229.8 3.2 fusion.35
  233.0 7.7 %collective-permute-start.32 = (bf16[192,4096]{1,0:T(8,128)(2,1)}, bf16[192,4096]{1,0:T(8,128)(2,1)S(1)}, u32[]{:S(2)}, u32[]{:S(2)}) collective-permute-start(bf16[192,4096]{1,0:T(8,128)(2,1)} %pad_maximum_fusion.1), channel_id=1, source_target_pairs={{0,2},{1,3},{2,0},{3,1},{4,6},{5,7},{6,4},{7,5},{8,10},{9,11},{10,... | collective-permute-start | bytes 4718600 | tf_op jit(solution)/shard_map/ppermute | solution.py:154
  241.7 3.9 collective-permute-done.25
  246.8 2.2 collective-permute-start.28
  249.2 3.7 convolution_convert_fusion
  256.5 2.0 fusion.36
  260.0 5.1 %convolution_convert_fusion.1 = bf16[256,4096]{1,0:T(8,128)(2,1)} fusion(bf16[896,4096]{0,1:T(8,128)(2,1)S(1)} %convert_bitcast_fusion, bf16[512,896]{1,0:T(8,128)(2,1)} %copy-done.18), kind=kOutput, calls=%fused_computation.24 | convolution fusion | flops 1880096768 | bytes 9895936 | tf_op jit(solution)/shard_map/dot_general | solution.py:131
  266.7 8.4 %collective-permute-start.37 = (bf16[192,4096]{1,0:T(8,128)(2,1)}, bf16[192,4096]{1,0:T(8,128)(2,1)S(1)}, u32[]{:S(2)}, u32[]{:S(2)}) collective-permute-start(bf16[192,4096]{1,0:T(8,128)(2,1)} %pad_maximum_fusion.2), channel_id=1, source_target_pairs={{0,2},{1,3},{2,0},{3,1},{4,6},{5,7},{6,4},{7,5},{8,10},{9,11},{10,... | collective-permute-start | bytes 4718600 | tf_op jit(solution)/shard_map/ppermute | solution.py:154
  276.7 1.9 slice_add_fusion.18
  280.1 1.8 collective-permute-start.33
  283.2 3.8 convolution_convert_fusion.10
  287.0 2.0 add.340
  293.6 2.6 convolution_convert_fusion.11
  297.9 3.9 collective-permute-start.41
  303.2 1.8 slice_add_fusion.26
  306.2 3.5 convolution_convert_fusion.16
  309.7 2.5 convolution_convert_fusion.17
  317.2 5.9 %collective-permute-start.45 = (bf16[144,4096]{1,0:T(8,128)(2,1)S(1)}, bf16[144,4096]{1,0:T(8,128)(2,1)S(1)}, u32[]{:S(2)}, u32[]{:S(2)}) collective-permute-start(bf16[144,4096]{1,0:T(8,128)(2,1)S(1)} %pad_maximum_fusion.4), channel_id=1, source_target_pairs={{0,2},{1,3},{2,0},{3,1},{4,6},{5,7},{6,4},{7,5},{8,10},{9,11},{10,... | collective-permute-start | bytes 3538952 | tf_op jit(solution)/shard_map/ppermute | solution.py:154
  327.1 18.1 %collective-permute-done.41 = bf16[192,4096]{1,0:T(8,128)(2,1)S(1)} collective-permute-done((bf16[192,4096]{1,0:T(8,128)(2,1)}, bf16[192,4096]{1,0:T(8,128)(2,1)S(1)}, u32[]{:S(2)}, u32[]{:S(2)}) %collective-permute-start.41) | collective-permute-done | bytes 1572896 | tf_op jit(solution)/shard_map/ppermute | solution.py:154
  347.1 2.4 convolution_convert_fusion.18
  349.6 7.0 %collective-permute-start.49 = (bf16[96,4096]{1,0:T(8,128)(2,1)S(1)}, bf16[96,4096]{1,0:T(8,128)(2,1)S(1)}, u32[]{:S(2)}, u32[]{:S(2)}) collective-permute-start(bf16[96,4096]{1,0:T(8,128)(2,1)S(1)} %slice_add_fusion.14), channel_id=1, source_target_pairs={{0,2},{1,3},{6,4},{7,5},{8,10},{9,11},{14,12},{15,13},{16,18},{17,... | collective-permute-start | bytes 2359304 | tf_op jit(solution)/shard_map/ppermute | solution.py:154
  358.2 2.4 convolution_convert_fusion.19
  362.5 19.0 %collective-permute-done.42 = bf16[64,4096]{1,0:T(8,128)(2,1)} collective-permute-done((bf16[64,4096]{1,0:T(8,128)(2,1)}, bf16[64,4096]{1,0:T(8,128)(2,1)}, u32[]{:S(2)}, u32[]{:S(2)}) %collective-permute-start.42) | collective-permute-done | bytes 524320 | tf_op jit(solution)/shard_map/ppermute | solution.py:174
  383.8 7.1 %collective-permute-start.52 = (bf16[48,4096]{1,0:T(8,128)(2,1)S(1)}, bf16[48,4096]{1,0:T(8,128)(2,1)S(1)}, u32[]{:S(2)}, u32[]{:S(2)}) collective-permute-start(bf16[48,4096]{1,0:T(8,128)(2,1)S(1)} %slice_add_fusion.25), channel_id=1, source_target_pairs={{0,2},{1,3},{6,4},{7,5},{8,10},{9,11},{14,12},{15,13},{16,18},{17,... | collective-permute-start | bytes 1179656 | tf_op jit(solution)/shard_map/ppermute | solution.py:154
  392.6 1.8 fusion.37
  394.4 2.6 collective-permute-done.46
  399.9 15.8 %collective-permute-done.48 = bf16[48,4096]{1,0:T(8,128)(2,1)S(1)} collective-permute-done((bf16[48,4096]{1,0:T(8,128)(2,1)S(1)}, bf16[48,4096]{1,0:T(8,128)(2,1)S(1)}, u32[]{:S(2)}, u32[]{:S(2)}) %collective-permute-start.48) | collective-permute-done | bytes 393248 | tf_op jit(solution)/shard_map/ppermute | solution.py:174
  418.2 9.8 %collective-permute-done.51 = bf16[32,4096]{1,0:T(8,128)(2,1)S(1)} collective-permute-done((bf16[32,4096]{1,0:T(8,128)(2,1)S(1)}, bf16[32,4096]{1,0:T(8,128)(2,1)S(1)}, u32[]{:S(2)}, u32[]{:S(2)}) %collective-permute-start.51) | collective-permute-done | bytes 262176 | tf_op jit(solution)/shard_map/ppermute | solution.py:174
  429.7 6.6 %collective-permute-done.54 = bf16[16,4096]{1,0:T(8,128)(2,1)S(1)} collective-permute-done((bf16[16,4096]{1,0:T(8,128)(2,1)S(1)}, bf16[16,4096]{1,0:T(8,128)(2,1)S(1)}, u32[]{:S(2)}, u32[]{:S(2)}) %collective-permute-start.54) | collective-permute-done | bytes 131104 | tf_op jit(solution)/shard_map/ppermute | solution.py:174
  (283 shorter events, 99.1 us)
Async XLA Ops:
  0.0 25.9 %copy-start = (bf16[896,896]{1,0:T(8,128)(2,1)S(1)}, bf16[896,896]{1,0:T(8,128)(2,1)}, u32[]{:S(2)}) copy-start(bf16[896,896]{1,0:T(8,128)(2,1)} %param.15) | copy-start | bytes 4816900
  2.1 9.8 %all-to-all-start = ((f32[4,2,128]{2,1,0:T(2,128)}), f32[4,2,128]{2,1,0:T(2,128)S(1)}, u32[]{:S(2)}, u32[]{:S(2)}) async-start(f32[4,2,128]{2,1,0:T(2,128)} %pad_maximum_fusion.5), calls=%async_computation | async-start | bytes 8192 | tf_op jit(solution)/shard_map/all_to_all | solution.py:27
  38.5 15.8 %collective-permute-start = (bf16[384,896]{1,0:T(8,128)(2,1)S(1)}, bf16[384,896]{1,0:T(8,128)(2,1)S(1)}, u32[]{:S(2)}, u32[]{:S(2)}) collective-permute-start(bf16[384,896]{1,0:T(8,128)(2,1)S(1)} %fusion.34), channel_id=1, source_target_pairs={{0,8},{8,0},{16,24},{24,16},{1,9},{9,1},{17,25},{25,17},{2,10},{10... | collective-permute-start | bytes 2064392 | tf_op jit(solution)/shard_map/ppermute | solution.py:114
  54.5 15.4 %collective-permute-start.1 = (bf16[384,896]{1,0:T(8,128)(2,1)S(1)}, bf16[384,896]{1,0:T(8,128)(2,1)S(1)}, u32[]{:S(2)}, u32[]{:S(2)}) collective-permute-start(bf16[384,896]{1,0:T(8,128)(2,1)S(1)} %add.297), channel_id=1, source_target_pairs={{0,16},{8,24},{16,0},{24,8},{1,17},{9,25},{17,1},{25,9},{2,18},{10... | collective-permute-start | bytes 2064392 | tf_op jit(solution)/shard_map/ppermute | solution.py:122
  56.0 15.4 %collective-permute-start.2 = (bf16[384,896]{1,0:T(8,128)(2,1)S(1)}, bf16[384,896]{1,0:T(8,128)(2,1)S(1)}, u32[]{:S(2)}, u32[]{:S(2)}) collective-permute-start(bf16[384,896]{1,0:T(8,128)(2,1)S(1)} %fusion.33), channel_id=1, source_target_pairs={{0,8},{8,0},{16,24},{24,16},{1,9},{9,1},{17,25},{25,17},{2,10},{10... | collective-permute-start | bytes 2064392 | tf_op jit(solution)/shard_map/ppermute | solution.py:114
  74.3 9.5 %collective-permute-start.3 = (bf16[192,4096]{1,0:T(8,128)(2,1)S(1)}, bf16[192,4096]{1,0:T(8,128)(2,1)S(1)}, u32[]{:S(2)}, u32[]{:S(2)}) collective-permute-start(bf16[192,4096]{1,0:T(8,128)(2,1)S(1)} %convolution_convert_fusion.14), channel_id=1, source_target_pairs={{0,1},{1,0},{2,3},{3,2},{4,5},{5,4},{6,7},{7,6},{8,9},{9,8},{10,11... | collective-permute-start | bytes 4718600 | tf_op jit(solution)/shard_map/ppermute | solution.py:135
  74.6 17.9 %collective-permute-start.4 = (bf16[384,896]{1,0:T(8,128)(2,1)S(1)}, bf16[384,896]{1,0:T(8,128)(2,1)S(1)}, u32[]{:S(2)}, u32[]{:S(2)}) collective-permute-start(bf16[384,896]{1,0:T(8,128)(2,1)S(1)} %add.301), channel_id=1, source_target_pairs={{0,16},{8,24},{16,0},{24,8},{1,17},{9,25},{17,1},{25,9},{2,18},{10... | collective-permute-start | bytes 2064392 | tf_op jit(solution)/shard_map/ppermute | solution.py:122
  75.0 22.5 %collective-permute-start.5 = (bf16[512,896]{1,0:T(8,128)(2,1)S(1)}, bf16[512,896]{1,0:T(8,128)(2,1)S(1)}, u32[]{:S(2)}, u32[]{:S(2)}) collective-permute-start(bf16[512,896]{1,0:T(8,128)(2,1)S(1)} %fusion.31), channel_id=1, source_target_pairs={{0,8},{8,0},{16,24},{24,16},{1,9},{9,1},{17,25},{25,17},{2,10},{10... | collective-permute-start | bytes 2752520 | tf_op jit(solution)/shard_map/ppermute | solution.py:114
  100.2 12.8 %collective-permute-start.7 = (bf16[192,4096]{1,0:T(8,128)(2,1)S(1)}, bf16[192,4096]{1,0:T(8,128)(2,1)S(1)}, u32[]{:S(2)}, u32[]{:S(2)}) collective-permute-start(bf16[192,4096]{1,0:T(8,128)(2,1)S(1)} %convolution_convert_fusion.12), channel_id=1, source_target_pairs={{0,1},{1,0},{2,3},{3,2},{4,5},{5,4},{6,7},{7,6},{8,9},{9,8},{10,11... | collective-permute-start | bytes 4718600 | tf_op jit(solution)/shard_map/ppermute | solution.py:135
  100.3 28.4 %collective-permute-start.6 = (bf16[144,4096]{1,0:T(8,128)(2,1)S(1)}, bf16[144,4096]{1,0:T(8,128)(2,1)S(1)}, u32[]{:S(2)}, u32[]{:S(2)}) collective-permute-start(bf16[144,4096]{1,0:T(8,128)(2,1)S(1)} %slice_add_fusion.7), channel_id=1, source_target_pairs={{0,2},{1,3},{2,0},{3,1},{4,6},{5,7},{6,4},{7,5},{8,10},{9,11},{10,... | collective-permute-start | bytes 3538952 | tf_op jit(solution)/shard_map/ppermute | solution.py:154
  102.2 22.5 %collective-permute-start.8 = (bf16[512,896]{1,0:T(8,128)(2,1)S(1)}, bf16[512,896]{1,0:T(8,128)(2,1)S(1)}, u32[]{:S(2)}, u32[]{:S(2)}) collective-permute-start(bf16[512,896]{1,0:T(8,128)(2,1)S(1)} %add.305), channel_id=1, source_target_pairs={{0,16},{8,24},{16,0},{24,8},{1,17},{9,25},{17,1},{25,9},{2,18},{10... | collective-permute-start | bytes 2752520 | tf_op jit(solution)/shard_map/ppermute | solution.py:122
  103.9 22.1 %collective-permute-start.9 = (bf16[512,896]{1,0:T(8,128)(2,1)S(1)}, bf16[512,896]{1,0:T(8,128)(2,1)S(1)}, u32[]{:S(2)}, u32[]{:S(2)}) collective-permute-start(bf16[512,896]{1,0:T(8,128)(2,1)S(1)} %fusion.30), channel_id=1, source_target_pairs={{0,8},{8,0},{16,24},{24,16},{1,9},{9,1},{17,25},{25,17},{2,10},{10... | collective-permute-start | bytes 2752520 | tf_op jit(solution)/shard_map/ppermute | solution.py:114
  128.7 32.6 %copy-start.12 = (bf16[144,4096]{1,0:T(8,128)(2,1)}, bf16[144,4096]{1,0:T(8,128)(2,1)S(1)}, u32[]{:S(2)}) copy-start(bf16[144,4096]{1,0:T(8,128)(2,1)S(1)} %collective-permute-done.6) | copy-start | bytes 3538948
  132.6 12.1 %collective-permute-start.10 = (bf16[256,4096]{1,0:T(8,128)(2,1)}, bf16[256,4096]{1,0:T(8,128)(2,1)S(1)}, u32[]{:S(2)}, u32[]{:S(2)}) collective-permute-start(bf16[256,4096]{1,0:T(8,128)(2,1)} %convolution_convert_fusion.8), channel_id=1, source_target_pairs={{0,1},{1,0},{2,3},{3,2},{4,5},{5,4},{6,7},{7,6},{8,9},{9,8},{10,11... | collective-permute-start | bytes 6291464 | tf_op jit(solution)/shard_map/ppermute | solution.py:135
  133.0 22.8 %collective-permute-start.11 = (bf16[512,896]{1,0:T(8,128)(2,1)S(1)}, bf16[512,896]{1,0:T(8,128)(2,1)S(1)}, u32[]{:S(2)}, u32[]{:S(2)}) collective-permute-start(bf16[512,896]{1,0:T(8,128)(2,1)S(1)} %add.309), channel_id=1, source_target_pairs={{0,16},{8,24},{16,0},{24,8},{1,17},{9,25},{17,1},{25,9},{2,18},{10... | collective-permute-start | bytes 2752520 | tf_op jit(solution)/shard_map/ppermute | solution.py:122
  134.8 22.5 %collective-permute-start.12 = (bf16[512,896]{1,0:T(8,128)(2,1)S(1)}, bf16[512,896]{1,0:T(8,128)(2,1)S(1)}, u32[]{:S(2)}, u32[]{:S(2)}) collective-permute-start(bf16[512,896]{1,0:T(8,128)(2,1)S(1)} %fusion.29), channel_id=1, source_target_pairs={{0,8},{8,0},{16,24},{24,16},{1,9},{9,1},{17,25},{25,17},{2,10},{10... | collective-permute-start | bytes 2752520 | tf_op jit(solution)/shard_map/ppermute | solution.py:114
  136.2 49.0 %collective-permute-start.17 = (bf16[144,4096]{1,0:T(8,128)(2,1)S(1)}, bf16[144,4096]{1,0:T(8,128)(2,1)S(1)}, u32[]{:S(2)}, u32[]{:S(2)}) collective-permute-start(bf16[144,4096]{1,0:T(8,128)(2,1)S(1)} %slice_add_fusion.6), channel_id=1, source_target_pairs={{0,2},{1,3},{2,0},{3,1},{4,6},{5,7},{6,4},{7,5},{8,10},{9,11},{10,... | collective-permute-start | bytes 3538952 | tf_op jit(solution)/shard_map/ppermute | solution.py:154
  161.3 10.0 %collective-permute-start.14 = (bf16[256,4096]{1,0:T(8,128)(2,1)}, bf16[256,4096]{1,0:T(8,128)(2,1)S(1)}, u32[]{:S(2)}, u32[]{:S(2)}) collective-permute-start(bf16[256,4096]{1,0:T(8,128)(2,1)} %convolution_convert_fusion.6), channel_id=1, source_target_pairs={{0,1},{1,0},{2,3},{3,2},{4,5},{5,4},{6,7},{7,6},{8,9},{9,8},{10,11... | collective-permute-start | bytes 6291464 | tf_op jit(solution)/shard_map/ppermute | solution.py:135
  161.4 14.6 %collective-permute-start.13 = (bf16[96,4096]{1,0:T(8,128)(2,1)S(1)}, bf16[96,4096]{1,0:T(8,128)(2,1)S(1)}, u32[]{:S(2)}, u32[]{:S(2)}) collective-permute-start(bf16[96,4096]{1,0:T(8,128)(2,1)S(1)} %slice_add_fusion.16), channel_id=1, source_target_pairs={{2,4},{3,5},{4,2},{5,3},{10,12},{11,13},{12,10},{13,11},{18,20},{1... | collective-permute-start | bytes 2359304 | tf_op jit(solution)/shard_map/ppermute | solution.py:169
  162.4 22.8 %collective-permute-start.15 = (bf16[512,896]{1,0:T(8,128)(2,1)S(1)}, bf16[512,896]{1,0:T(8,128)(2,1)S(1)}, u32[]{:S(2)}, u32[]{:S(2)}) collective-permute-start(bf16[512,896]{1,0:T(8,128)(2,1)S(1)} %add.314), channel_id=1, source_target_pairs={{0,16},{8,24},{16,0},{24,8},{1,17},{9,25},{17,1},{25,9},{2,18},{10... | collective-permute-start | bytes 2752520 | tf_op jit(solution)/shard_map/ppermute | solution.py:122
  162.8 22.5 %collective-permute-start.16 = (bf16[512,896]{1,0:T(8,128)(2,1)S(1)}, bf16[512,896]{1,0:T(8,128)(2,1)S(1)}, u32[]{:S(2)}, u32[]{:S(2)}) collective-permute-start(bf16[512,896]{1,0:T(8,128)(2,1)S(1)} %fusion.28), channel_id=1, source_target_pairs={{0,8},{8,0},{16,24},{24,16},{1,9},{9,1},{17,25},{25,17},{2,10},{10... | collective-permute-start | bytes 2752520 | tf_op jit(solution)/shard_map/ppermute | solution.py:114
  171.4 45.1 %collective-permute-start.22 = (bf16[192,4096]{1,0:T(8,128)(2,1)S(1)}, bf16[192,4096]{1,0:T(8,128)(2,1)S(1)}, u32[]{:S(2)}, u32[]{:S(2)}) collective-permute-start(bf16[192,4096]{1,0:T(8,128)(2,1)S(1)} %slice_add_fusion.4), channel_id=1, source_target_pairs={{0,2},{1,3},{2,0},{3,1},{4,6},{5,7},{6,4},{7,5},{8,10},{9,11},{10,... | collective-permute-start | bytes 4718600 | tf_op jit(solution)/shard_map/ppermute | solution.py:154
  176.0 19.6 %copy-start.21 = (bf16[96,4096]{1,0:T(8,128)(2,1)}, bf16[96,4096]{1,0:T(8,128)(2,1)S(1)}, u32[]{:S(2)}) copy-start(bf16[96,4096]{1,0:T(8,128)(2,1)S(1)} %collective-permute-done.13) | copy-start | bytes 2359300
  186.4 23.3 %collective-permute-start.18 = (bf16[96,4096]{1,0:T(8,128)(2,1)}, bf16[96,4096]{1,0:T(8,128)(2,1)}, u32[]{:S(2)}, u32[]{:S(2)}) collective-permute-start(bf16[96,4096]{1,0:T(8,128)(2,1)} %slice_add_fusion.15), channel_id=1, source_target_pairs={{2,4},{3,5},{4,2},{5,3},{10,12},{11,13},{12,10},{13,11},{18,20},{1... | collective-permute-start | bytes 2359304 | tf_op jit(solution)/shard_map/ppermute | solution.py:169
  192.1 11.7 %collective-permute-start.19 = (bf16[256,4096]{1,0:T(8,128)(2,1)}, bf16[256,4096]{1,0:T(8,128)(2,1)S(1)}, u32[]{:S(2)}, u32[]{:S(2)}) collective-permute-start(bf16[256,4096]{1,0:T(8,128)(2,1)} %convolution_convert_fusion.4), channel_id=1, source_target_pairs={{0,1},{1,0},{2,3},{3,2},{4,5},{5,4},{6,7},{7,6},{8,9},{9,8},{10,11... | collective-permute-start | bytes 6291464 | tf_op jit(solution)/shard_map/ppermute | solution.py:135
  192.3 22.8 %collective-permute-start.20 = (bf16[512,896]{1,0:T(8,128)(2,1)S(1)}, bf16[512,896]{1,0:T(8,128)(2,1)S(1)}, u32[]{:S(2)}, u32[]{:S(2)}) collective-permute-start(bf16[512,896]{1,0:T(8,128)(2,1)S(1)} %add.319), channel_id=1, source_target_pairs={{0,16},{8,24},{16,0},{24,8},{1,17},{9,25},{17,1},{25,9},{2,18},{10... | collective-permute-start | bytes 2752520 | tf_op jit(solution)/shard_map/ppermute | solution.py:122
  194.0 22.5 %collective-permute-start.21 = (bf16[512,896]{1,0:T(8,128)(2,1)S(1)}, bf16[512,896]{1,0:T(8,128)(2,1)S(1)}, u32[]{:S(2)}, u32[]{:S(2)}) collective-permute-start(bf16[512,896]{1,0:T(8,128)(2,1)S(1)} %fusion.27), channel_id=1, source_target_pairs={{0,8},{8,0},{16,24},{24,16},{1,9},{9,1},{17,25},{25,17},{2,10},{10... | collective-permute-start | bytes 2752520 | tf_op jit(solution)/shard_map/ppermute | solution.py:114
  203.8 41.7 %collective-permute-start.27 = (bf16[192,4096]{1,0:T(8,128)(2,1)}, bf16[192,4096]{1,0:T(8,128)(2,1)S(1)}, u32[]{:S(2)}, u32[]{:S(2)}) collective-permute-start(bf16[192,4096]{1,0:T(8,128)(2,1)} %pad_maximum_fusion), channel_id=1, source_target_pairs={{0,2},{1,3},{2,0},{3,1},{4,6},{5,7},{6,4},{7,5},{8,10},{9,11},{10,... | collective-permute-start | bytes 4718600 | tf_op jit(solution)/shard_map/ppermute | solution.py:154
  216.6 28.9 %collective-permute-start.23 = (bf16[128,4096]{1,0:T(8,128)(2,1)S(1)}, bf16[128,4096]{1,0:T(8,128)(2,1)S(1)}, u32[]{:S(2)}, u32[]{:S(2)}) collective-permute-start(bf16[128,4096]{1,0:T(8,128)(2,1)S(1)} %slice_add_fusion.12), channel_id=1, source_target_pairs={{2,4},{3,5},{4,2},{5,3},{10,12},{11,13},{12,10},{13,11},{18,20},{1... | collective-permute-start | bytes 3145736 | tf_op jit(solution)/shard_map/ppermute | solution.py:169
  222.5 10.5 %collective-permute-start.24 = (bf16[256,4096]{1,0:T(8,128)(2,1)}, bf16[256,4096]{1,0:T(8,128)(2,1)S(1)}, u32[]{:S(2)}, u32[]{:S(2)}) collective-permute-start(bf16[256,4096]{1,0:T(8,128)(2,1)} %convolution_convert_fusion.2), channel_id=1, source_target_pairs={{0,1},{1,0},{2,3},{3,2},{4,5},{5,4},{6,7},{7,6},{8,9},{9,8},{10,11... | collective-permute-start | bytes 6291464 | tf_op jit(solution)/shard_map/ppermute | solution.py:135
  222.7 22.8 %collective-permute-start.25 = (bf16[512,896]{1,0:T(8,128)(2,1)S(1)}, bf16[512,896]{1,0:T(8,128)(2,1)S(1)}, u32[]{:S(2)}, u32[]{:S(2)}) collective-permute-start(bf16[512,896]{1,0:T(8,128)(2,1)S(1)} %add.324), channel_id=1, source_target_pairs={{0,16},{8,24},{16,0},{24,8},{1,17},{9,25},{17,1},{25,9},{2,18},{10... | collective-permute-start | bytes 2752520 | tf_op jit(solution)/shard_map/ppermute | solution.py:122
  223.1 18.5 %collective-permute-start.26 = (bf16[384,896]{1,0:T(8,128)(2,1)}, bf16[384,896]{1,0:T(8,128)(2,1)}, u32[]{:S(2)}, u32[]{:S(2)}) collective-permute-start(bf16[384,896]{1,0:T(8,128)(2,1)} %fusion.32), channel_id=1, source_target_pairs={{0,8},{8,0},{16,24},{24,16},{1,9},{9,1},{17,25},{25,17},{2,10},{10... | collective-permute-start | bytes 2064392 | tf_op jit(solution)/shard_map/ppermute | solution.py:114
  233.0 45.6 %collective-permute-start.32 = (bf16[192,4096]{1,0:T(8,128)(2,1)}, bf16[192,4096]{1,0:T(8,128)(2,1)S(1)}, u32[]{:S(2)}, u32[]{:S(2)}) collective-permute-start(bf16[192,4096]{1,0:T(8,128)(2,1)} %pad_maximum_fusion.1), channel_id=1, source_target_pairs={{0,2},{1,3},{2,0},{3,1},{4,6},{5,7},{6,4},{7,5},{8,10},{9,11},{10,... | collective-permute-start | bytes 4718600 | tf_op jit(solution)/shard_map/ppermute | solution.py:154
  246.8 31.9 %collective-permute-start.28 = (bf16[128,4096]{1,0:T(8,128)(2,1)}, bf16[128,4096]{1,0:T(8,128)(2,1)}, u32[]{:S(2)}, u32[]{:S(2)}) collective-permute-start(bf16[128,4096]{1,0:T(8,128)(2,1)} %slice_add_fusion.11), channel_id=1, source_target_pairs={{2,4},{3,5},{4,2},{5,3},{10,12},{11,13},{12,10},{13,11},{18,20},{1... | collective-permute-start | bytes 3145736 | tf_op jit(solution)/shard_map/ppermute | solution.py:169
  252.9 13.9 %collective-permute-start.29 = (bf16[256,4096]{1,0:T(8,128)(2,1)}, bf16[256,4096]{1,0:T(8,128)(2,1)}, u32[]{:S(2)}, u32[]{:S(2)}) collective-permute-start(bf16[256,4096]{1,0:T(8,128)(2,1)} %convolution_convert_fusion), channel_id=1, source_target_pairs={{0,1},{1,0},{2,3},{3,2},{4,5},{5,4},{6,7},{7,6},{8,9},{9,8},{10,11... | collective-permute-start | bytes 6291464 | tf_op jit(solution)/shard_map/ppermute | solution.py:135
  254.3 24.3 %collective-permute-start.30 = (bf16[384,896]{1,0:T(8,128)(2,1)S(1)}, bf16[384,896]{1,0:T(8,128)(2,1)}, u32[]{:S(2)}, u32[]{:S(2)}) collective-permute-start(bf16[384,896]{1,0:T(8,128)(2,1)S(1)} %add.332), channel_id=1, source_target_pairs={{0,16},{8,24},{16,0},{24,8},{1,17},{9,25},{17,1},{25,9},{2,18},{10... | collective-permute-start | bytes 2064392 | tf_op jit(solution)/shard_map/ppermute | solution.py:122
  255.0 23.6 %collective-permute-start.31 = (bf16[256,896]{1,0:T(8,128)(2,1)}, bf16[256,896]{1,0:T(8,128)(2,1)}, u32[]{:S(2)}, u32[]{:S(2)}) collective-permute-start(bf16[256,896]{1,0:T(8,128)(2,1)} %fusion.35), channel_id=1, source_target_pairs={{0,8},{8,0},{16,24},{24,16},{1,9},{9,1},{17,25},{25,17},{2,10},{10... | collective-permute-start | bytes 1376264 | tf_op jit(solution)/shard_map/ppermute | solution.py:114
  266.7 45.5 %collective-permute-start.37 = (bf16[192,4096]{1,0:T(8,128)(2,1)}, bf16[192,4096]{1,0:T(8,128)(2,1)S(1)}, u32[]{:S(2)}, u32[]{:S(2)}) collective-permute-start(bf16[192,4096]{1,0:T(8,128)(2,1)} %pad_maximum_fusion.2), channel_id=1, source_target_pairs={{0,2},{1,3},{2,0},{3,1},{4,6},{5,7},{6,4},{7,5},{8,10},{9,11},{10,... | collective-permute-start | bytes 4718600 | tf_op jit(solution)/shard_map/ppermute | solution.py:154
  280.1 24.8 %collective-permute-start.33 = (bf16[128,4096]{1,0:T(8,128)(2,1)}, bf16[128,4096]{1,0:T(8,128)(2,1)}, u32[]{:S(2)}, u32[]{:S(2)}) collective-permute-start(bf16[128,4096]{1,0:T(8,128)(2,1)} %slice_add_fusion.10), channel_id=1, source_target_pairs={{2,4},{3,5},{4,2},{5,3},{10,12},{11,13},{12,10},{13,11},{18,20},{1... | collective-permute-start | bytes 3145736 | tf_op jit(solution)/shard_map/ppermute | solution.py:169
  287.0 10.8 %collective-permute-start.34 = (bf16[192,4096]{1,0:T(8,128)(2,1)}, bf16[192,4096]{1,0:T(8,128)(2,1)}, u32[]{:S(2)}, u32[]{:S(2)}) collective-permute-start(bf16[192,4096]{1,0:T(8,128)(2,1)} %convolution_convert_fusion.10), channel_id=1, source_target_pairs={{0,1},{1,0},{2,3},{3,2},{4,5},{5,4},{6,7},{7,6},{8,9},{9,8},{10,11... | collective-permute-start | bytes 4718600 | tf_op jit(solution)/shard_map/ppermute | solution.py:135
  289.1 15.9 %collective-permute-start.35 = (bf16[256,896]{1,0:T(8,128)(2,1)}, bf16[256,896]{1,0:T(8,128)(2,1)}, u32[]{:S(2)}, u32[]{:S(2)}) collective-permute-start(bf16[256,896]{1,0:T(8,128)(2,1)} %add.340), channel_id=1, source_target_pairs={{0,16},{8,24},{16,0},{24,8},{1,17},{9,25},{17,1},{25,9},{2,18},{10... | collective-permute-start | bytes 1376264 | tf_op jit(solution)/shard_map/ppermute | solution.py:122
  290.6 14.4 %collective-permute-start.36 = (bf16[128,896]{1,0:T(8,128)(2,1)}, bf16[128,896]{1,0:T(8,128)(2,1)}, u32[]{:S(2)}, u32[]{:S(2)}) collective-permute-start(bf16[128,896]{1,0:T(8,128)(2,1)} %fusion.36), channel_id=1, source_target_pairs={{0,8},{8,0},{16,24},{24,16},{1,9},{9,1},{17,25},{25,17},{2,10},{10... | collective-permute-start | bytes 688136 | tf_op jit(solution)/shard_map/ppermute | solution.py:114
  297.9 47.4 %collective-permute-start.41 = (bf16[192,4096]{1,0:T(8,128)(2,1)}, bf16[192,4096]{1,0:T(8,128)(2,1)S(1)}, u32[]{:S(2)}, u32[]{:S(2)}) collective-permute-start(bf16[192,4096]{1,0:T(8,128)(2,1)} %pad_maximum_fusion.3), channel_id=1, source_target_pairs={{0,2},{1,3},{2,0},{3,1},{4,6},{5,7},{6,4},{7,5},{8,10},{9,11},{10,... | collective-permute-start | bytes 4718600 | tf_op jit(solution)/shard_map/ppermute | solution.py:154
  312.3 12.6 %collective-permute-start.38 = (bf16[128,4096]{1,0:T(8,128)(2,1)S(1)}, bf16[128,4096]{1,0:T(8,128)(2,1)S(1)}, u32[]{:S(2)}, u32[]{:S(2)}) collective-permute-start(bf16[128,4096]{1,0:T(8,128)(2,1)S(1)} %slice_add_fusion.9), channel_id=1, source_target_pairs={{2,4},{3,5},{4,2},{5,3},{10,12},{11,13},{12,10},{13,11},{18,20},{1... | collective-permute-start | bytes 3145736 | tf_op jit(solution)/shard_map/ppermute | solution.py:169
  313.1 11.7 %collective-permute-start.39 = (bf16[128,4096]{1,0:T(8,128)(2,1)}, bf16[128,4096]{1,0:T(8,128)(2,1)S(1)}, u32[]{:S(2)}, u32[]{:S(2)}) collective-permute-start(bf16[128,4096]{1,0:T(8,128)(2,1)} %convolution_convert_fusion.16), channel_id=1, source_target_pairs={{0,1},{1,0},{2,3},{3,2},{4,5},{5,4},{6,7},{7,6},{8,9},{9,8},{10,11... | collective-permute-start | bytes 3145736 | tf_op jit(solution)/shard_map/ppermute | solution.py:135
  314.2 10.6 %collective-permute-start.40 = (bf16[128,896]{1,0:T(8,128)(2,1)S(1)}, bf16[128,896]{1,0:T(8,128)(2,1)S(1)}, u32[]{:S(2)}, u32[]{:S(2)}) collective-permute-start(bf16[128,896]{1,0:T(8,128)(2,1)S(1)} %add.348), channel_id=1, source_target_pairs={{0,16},{8,24},{16,0},{24,8},{1,17},{9,25},{17,1},{25,9},{2,18},{10... | collective-permute-start | bytes 688136 | tf_op jit(solution)/shard_map/ppermute | solution.py:122
  317.2 65.7 %collective-permute-start.45 = (bf16[144,4096]{1,0:T(8,128)(2,1)S(1)}, bf16[144,4096]{1,0:T(8,128)(2,1)S(1)}, u32[]{:S(2)}, u32[]{:S(2)}) collective-permute-start(bf16[144,4096]{1,0:T(8,128)(2,1)S(1)} %pad_maximum_fusion.4), channel_id=1, source_target_pairs={{0,2},{1,3},{2,0},{3,1},{4,6},{5,7},{6,4},{7,5},{8,10},{9,11},{10,... | collective-permute-start | bytes 3538952 | tf_op jit(solution)/shard_map/ppermute | solution.py:154
  324.9 21.4 %copy-start.16 = (bf16[128,4096]{1,0:T(8,128)(2,1)}, bf16[128,4096]{1,0:T(8,128)(2,1)S(1)}, u32[]{:S(2)}) copy-start(bf16[128,4096]{1,0:T(8,128)(2,1)S(1)} %collective-permute-done.38) | copy-start | bytes 3145732
  325.8 55.6 %collective-permute-start.42 = (bf16[64,4096]{1,0:T(8,128)(2,1)}, bf16[64,4096]{1,0:T(8,128)(2,1)}, u32[]{:S(2)}, u32[]{:S(2)}) collective-permute-start(bf16[64,4096]{1,0:T(8,128)(2,1)} %slice_add_fusion.24), channel_id=1, source_target_pairs={{2,0},{3,1},{4,6},{5,7},{10,8},{11,9},{12,14},{13,15},{18,16},{19,... | collective-permute-start | bytes 1572872 | tf_op jit(solution)/shard_map/ppermute | solution.py:174
  346.3 35.2 %collective-permute-start.43 = (bf16[128,4096]{1,0:T(8,128)(2,1)}, bf16[128,4096]{1,0:T(8,128)(2,1)S(1)}, u32[]{:S(2)}, u32[]{:S(2)}) collective-permute-start(bf16[128,4096]{1,0:T(8,128)(2,1)} %slice_add_fusion.8), channel_id=1, source_target_pairs={{2,4},{3,5},{4,2},{5,3},{10,12},{11,13},{12,10},{13,11},{18,20},{1... | collective-permute-start | bytes 3145736 | tf_op jit(solution)/shard_map/ppermute | solution.py:169
  349.5 11.1 %collective-permute-start.44 = (bf16[64,4096]{1,0:T(8,128)(2,1)S(1)}, bf16[64,4096]{1,0:T(8,128)(2,1)S(1)}, u32[]{:S(2)}, u32[]{:S(2)}) collective-permute-start(bf16[64,4096]{1,0:T(8,128)(2,1)S(1)} %convolution_convert_fusion.18), channel_id=1, source_target_pairs={{0,1},{1,0},{2,3},{3,2},{4,5},{5,4},{6,7},{7,6},{8,9},{9,8},{10,11... | collective-permute-start | bytes 1572872 | tf_op jit(solution)/shard_map/ppermute | solution.py:135
  349.6 48.8 %collective-permute-start.49 = (bf16[96,4096]{1,0:T(8,128)(2,1)S(1)}, bf16[96,4096]{1,0:T(8,128)(2,1)S(1)}, u32[]{:S(2)}, u32[]{:S(2)}) collective-permute-start(bf16[96,4096]{1,0:T(8,128)(2,1)S(1)} %slice_add_fusion.14), channel_id=1, source_target_pairs={{0,2},{1,3},{6,4},{7,5},{8,10},{9,11},{14,12},{15,13},{16,18},{17,... | collective-permute-start | bytes 2359304 | tf_op jit(solution)/shard_map/ppermute | solution.py:154
  361.4 29.5 %copy-start.6 = (bf16[64,4096]{1,0:T(8,128)(2,1)S(1)}, bf16[64,4096]{1,0:T(8,128)(2,1)}, u32[]{:S(2)}) copy-start(bf16[64,4096]{1,0:T(8,128)(2,1)} %slice_add_fusion.19) | copy-start | bytes 1572868
  361.4 29.5 %copy-start.17 = (bf16[128,4096]{1,0:T(8,128)(2,1)S(1)}, bf16[128,4096]{1,0:T(8,128)(2,1)}, u32[]{:S(2)}) copy-start(bf16[128,4096]{1,0:T(8,128)(2,1)} %copy-done.16) | copy-start | bytes 3145732
  381.6 15.4 %collective-permute-start.46 = (bf16[64,4096]{1,0:T(8,128)(2,1)S(1)}, bf16[64,4096]{1,0:T(8,128)(2,1)S(1)}, u32[]{:S(2)}, u32[]{:S(2)}) collective-permute-start(bf16[64,4096]{1,0:T(8,128)(2,1)S(1)} %slice_add_fusion.23), channel_id=1, source_target_pairs={{2,0},{3,1},{4,6},{5,7},{10,8},{11,9},{12,14},{13,15},{18,16},{19,... | collective-permute-start | bytes 1572872 | tf_op jit(solution)/shard_map/ppermute | solution.py:174
  383.0 14.0 %collective-permute-start.47 = (bf16[96,4096]{1,0:T(8,128)(2,1)S(1)}, bf16[96,4096]{1,0:T(8,128)(2,1)S(1)}, u32[]{:S(2)}, u32[]{:S(2)}) collective-permute-start(bf16[96,4096]{1,0:T(8,128)(2,1)S(1)} %slice_add_fusion.13), channel_id=1, source_target_pairs={{2,4},{3,5},{4,2},{5,3},{10,12},{11,13},{12,10},{13,11},{18,20},{1... | collective-permute-start | bytes 2359304 | tf_op jit(solution)/shard_map/ppermute | solution.py:169
  383.8 33.2 %collective-permute-start.52 = (bf16[48,4096]{1,0:T(8,128)(2,1)S(1)}, bf16[48,4096]{1,0:T(8,128)(2,1)S(1)}, u32[]{:S(2)}, u32[]{:S(2)}) collective-permute-start(bf16[48,4096]{1,0:T(8,128)(2,1)S(1)} %slice_add_fusion.25), channel_id=1, source_target_pairs={{0,2},{1,3},{6,4},{7,5},{8,10},{9,11},{14,12},{15,13},{16,18},{17,... | collective-permute-start | bytes 1179656 | tf_op jit(solution)/shard_map/ppermute | solution.py:154
  397.1 18.6 %collective-permute-start.48 = (bf16[48,4096]{1,0:T(8,128)(2,1)S(1)}, bf16[48,4096]{1,0:T(8,128)(2,1)S(1)}, u32[]{:S(2)}, u32[]{:S(2)}) collective-permute-start(bf16[48,4096]{1,0:T(8,128)(2,1)S(1)} %slice_add_fusion.29), channel_id=1, source_target_pairs={{2,0},{3,1},{4,6},{5,7},{10,8},{11,9},{12,14},{13,15},{18,16},{19,... | collective-permute-start | bytes 1179656 | tf_op jit(solution)/shard_map/ppermute | solution.py:174
  398.4 19.3 %copy-start.11 = (bf16[48,4096]{1,0:T(8,128)(2,1)S(1)}, bf16[48,4096]{1,0:T(8,128)(2,1)}, u32[]{:S(2)}) copy-start(bf16[48,4096]{1,0:T(8,128)(2,1)} %slice_add_fusion.26) | copy-start | bytes 1179652
  398.4 17.2 %collective-permute-start.50 = (bf16[64,4096]{1,0:T(8,128)(2,1)S(1)}, bf16[64,4096]{1,0:T(8,128)(2,1)S(1)}, u32[]{:S(2)}, u32[]{:S(2)}) collective-permute-start(bf16[64,4096]{1,0:T(8,128)(2,1)S(1)} %slice_add_fusion.17), channel_id=1, source_target_pairs={{2,4},{3,5},{4,2},{5,3},{10,12},{11,13},{12,10},{13,11},{18,20},{1... | collective-permute-start | bytes 1572872 | tf_op jit(solution)/shard_map/ppermute | solution.py:169
  415.7 12.3 %collective-permute-start.51 = (bf16[32,4096]{1,0:T(8,128)(2,1)S(1)}, bf16[32,4096]{1,0:T(8,128)(2,1)S(1)}, u32[]{:S(2)}, u32[]{:S(2)}) collective-permute-start(bf16[32,4096]{1,0:T(8,128)(2,1)S(1)} %slice_add_fusion.32), channel_id=1, source_target_pairs={{2,0},{3,1},{4,6},{5,7},{10,8},{11,9},{12,14},{13,15},{18,16},{19,... | collective-permute-start | bytes 786440 | tf_op jit(solution)/shard_map/ppermute | solution.py:174
  417.1 11.0 %collective-permute-start.53 = (bf16[32,4096]{1,0:T(8,128)(2,1)S(1)}, bf16[32,4096]{1,0:T(8,128)(2,1)S(1)}, u32[]{:S(2)}, u32[]{:S(2)}) collective-permute-start(bf16[32,4096]{1,0:T(8,128)(2,1)S(1)} %slice_add_fusion.30), channel_id=1, source_target_pairs={{2,4},{3,5},{4,2},{5,3},{10,12},{11,13},{12,10},{13,11},{18,20},{1... | collective-permute-start | bytes 786440 | tf_op jit(solution)/shard_map/ppermute | solution.py:169
  417.8 20.3 %copy-start.1 = (bf16[896,896]{1,0:T(8,128)(2,1)S(1)}, bf16[896,896]{1,0:T(8,128)(2,1)}, u32[]{:S(2)}) copy-start(bf16[896,896]{1,0:T(8,128)(2,1)} %param.15) | copy-start | bytes 4816900
  428.1 8.2 %collective-permute-start.54 = (bf16[16,4096]{1,0:T(8,128)(2,1)S(1)}, bf16[16,4096]{1,0:T(8,128)(2,1)S(1)}, u32[]{:S(2)}, u32[]{:S(2)}) collective-permute-start(bf16[16,4096]{1,0:T(8,128)(2,1)S(1)} %slice_add_fusion.34), channel_id=1, source_target_pairs={{2,0},{3,1},{4,6},{5,7},{10,8},{11,9},{12,14},{13,15},{18,16},{19,... | collective-permute-start | bytes 393224 | tf_op jit(solution)/shard_map/ppermute | solution.py:174
  (24 other events, 108.3 us)
where the time goes:
time: 447 us; the launch traced here: 438 us
  waiting for transfers between devices  154 us (34%)
  matrix products  123 us (28%)
  starting transfers between devices  101 us (23%)
  other arithmetic  52.4 us (12%)
  local copies, waits for them, and re-layouts  6.15 us (1%)
    dot_general x20, matrix products, multiply(): jnp.dot(picked, shared['solved'], preferred_element_type=jnp.float32)  60.5 us
    ppermute x10, waiting for transfers between devices, share_again(): s['rows_in'] = lax.ppermute(s['rows'], 'row', along_y)  55.6 us
    ppermute x5, waiting for transfers between devices, move_out(): s['from_inner'] = lax.ppermute(leaving(k), 'col', outward)  53.8 us
    ppermute x10, starting transfers between devices, move_in(): come = lax.ppermute(sent, 'col', ends if k < count - ALONE else inward)  52.5 us
    dot_general x10, matrix products, pick(): lax.dot_general(onehot, shared['solved'], (((1,), (1,)), ((), ())), prefe...  39.5 us
    ppermute x10, waiting for transfers between devices, share(): s['rows_in'] = lax.ppermute(s['rows'], 'row', along_x)  22.4 us
    ppermute x10, waiting for transfers between devices, move_in(): come = lax.ppermute(sent, 'col', ends if k < count - ALONE else inward)  20.8 us
    dot_general x1, matrix products, add_throats(): summed = jnp.dot(left, right, preferred_element_type=jnp.float32)  13.9 us
  transfers between devices with their start and end apart: 56, of which 22 were waited for; matrix products, arithmetic and copies ran while one was open for 32% of the time, Pallas kernels for 0%

commit v1 on v0

--- a/solution.py
+++ b/solution.py
@@ -6,7 +6,7 @@
 STEPS = (3, 3, 4, 4, 4, 4, 4, 3, 2, 1)
 LATER = 3
 STAYS = 1
-ALONE = 2
+ALONE = 1
 
 
 def route_throats(owners, interior, offset, conductance, row_count, owner_width):

time: 447 us -> 442 us (0.989)
  waiting for transfers between devices: 154 us -> 149 us
    ppermute x5 -> x4, waiting for transfers between devices: 53.8 us -> 39.6 us  [move_out(): s['from_inner'] = lax.ppermute(leaving(k), 'col', outward)]
    ppermute x10, waiting for transfers between devices: 20.8 us -> 29.4 us  [move_in(): come = lax.ppermute(sent, 'col', ends if k < count - ALONE else inward)]
  transfers between devices with their start and end apart: 56 -> 55, of which waited for: 22 -> 22; matrix products, arithmetic and copies ran while one was open for 32% -> 33% of each run, Pallas kernels for 0% -> 0%
where the time goes in v1:
time: 442 us; the launch traced here: 434 us
  waiting for transfers between devices  149 us (34%)
  matrix products  124 us (28%)
  starting transfers between devices  101 us (23%)
  other arithmetic  53.6 us (12%)
  local copies, waits for them, and re-layouts  5.34 us (1%)
    dot_general x20, matrix products, multiply(): jnp.dot(picked, shared['solved'], preferred_element_type=jnp.float32)  61.4 us
    ppermute x10, waiting for transfers between devices, share_again(): s['rows_in'] = lax.ppermute(s['rows'], 'row', along_y)  55.6 us
    ppermute x10, starting transfers between devices, move_in(): come = lax.ppermute(sent, 'col', ends if k < count - ALONE else inward)  52.7 us
    ppermute x4, waiting for transfers between devices, move_out(): s['from_inner'] = lax.ppermute(leaving(k), 'col', outward)  39.6 us
    dot_general x10, matrix products, pick(): lax.dot_general(onehot, shared['solved'], (((1,), (1,)), ((), ())), prefe...  39.5 us
    ppermute x10, waiting for transfers between devices, move_in(): come = lax.ppermute(sent, 'col', ends if k < count - ALONE else inward)  29.4 us
    ppermute x10, waiting for transfers between devices, share(): s['rows_in'] = lax.ppermute(s['rows'], 'row', along_x)  22.4 us
    dot_general x1, matrix products, add_throats(): summed = jnp.dot(left, right, preferred_element_type=jnp.float32)  13.9 us
  transfers between devices with their start and end apart: 55, of which 22 were waited for; matrix products, arithmetic and copies ran while one was open for 33% of the time, Pallas kernels for 0%

profile of v1, /device:TPU:0, one launch (start us, length us, event | category | flops | bytes accessed | tf_op | source)
XLA Modules:
  0.0 433.9 jit_solution(7342158632919163317)
XLA Ops:
  2.1 5.2 %all-to-all-start = ((f32[4,2,128]{2,1,0:T(2,128)}), f32[4,2,128]{2,1,0:T(2,128)S(1)}, u32[]{:S(2)}, u32[]{:S(2)}) async-start(f32[4,2,128]{2,1,0:T(2,128)} %pad_maximum_fusion.6), calls=%async_computation | async-start | bytes 8192 | tf_op jit(solution)/shard_map/all_to_all | solution.py:27
  12.0 13.9 %add_convert_fusion.7 = bf16[896,4096]{1,0:T(8,128)(2,1)S(1)} fusion(bf16[896,4096]{1,0:T(8,128)(2,1)} %param.13, s32[1024]{0:T(1024)S(1)} %pad_add_fusion.1, s32[1024]{0:T(1024)S(1)} %pad_add_fusion, bf16[1024]{0:T(1024)(128)(2,1)S(1)} %pad_maximum_fusion.7), kind=kOutput, calls=%fused_computation.3.clone.clone.clone.clone.1 | convolution fusion | flops 7533232128 | bytes 14690304 | tf_op jit(solution)/shard_map/dot_general | solution.py:43
  25.9 9.1 %convert_bitcast_fusion = bf16[896,4096]{0,1:T(8,128)(2,1)S(1)} fusion(bf16[896,896]{1,0:T(8,128)(2,1)S(1)} %copy-done, bf16[896,4096]{1,0:T(8,128)(2,1)S(1)} %add_convert_fusion.7), kind=kOutput, calls=%fused_computation.16 | convolution fusion | flops 6580338688 | bytes 16285696 | tf_op jit(solution)/shard_map/dot_general | solution.py:78
  35.0 3.5 fusion.34
  39.1 3.5 fusion.33
  42.6 11.7 %collective-permute-done = bf16[384,896]{1,0:T(8,128)(2,1)S(1)} collective-permute-done((bf16[384,896]{1,0:T(8,128)(2,1)S(1)}, bf16[384,896]{1,0:T(8,128)(2,1)S(1)}, u32[]{:S(2)}, u32[]{:S(2)}) %collective-permute-start) | collective-permute-done | bytes 688160 | tf_op jit(solution)/shard_map/ppermute | solution.py:114
  57.4 4.5 %fusion.31 = bf16[512,896]{1,0:T(8,128)(2,1)S(1)} fusion(bf16[896,4096]{0,1:T(8,128)(2,1)S(1)} %convert_bitcast_fusion, s32[512]{0:T(512)S(1)} %pad_add_fusion.4), kind=kOutput, calls=%fused_computation.72 | convolution fusion | flops 3760652288 | bytes 8259584 | tf_op jit(solution)/shard_map/dot_general | solution.py:107
  62.0 7.9 %collective-permute-done.1 = bf16[384,896]{1,0:T(8,128)(2,1)S(1)} collective-permute-done((bf16[384,896]{1,0:T(8,128)(2,1)S(1)}, bf16[384,896]{1,0:T(8,128)(2,1)S(1)}, u32[]{:S(2)}, u32[]{:S(2)}) %collective-permute-start.1) | collective-permute-done | bytes 688160 | tf_op jit(solution)/shard_map/ppermute | solution.py:122
  71.5 2.6 convolution_convert_fusion.14
  76.7 2.6 convolution_convert_fusion.15
  79.3 4.5 %fusion.30 = bf16[512,896]{1,0:T(8,128)(2,1)S(1)} fusion(bf16[896,4096]{0,1:T(8,128)(2,1)S(1)} %convert_bitcast_fusion, s32[512]{0:T(512)S(1)} %pad_add_fusion.5), kind=kOutput, calls=%fused_computation.71 | convolution fusion | flops 3760652288 | bytes 8259584 | tf_op jit(solution)/shard_map/dot_general | solution.py:107
  84.0 8.5 %collective-permute-done.4 = bf16[384,896]{1,0:T(8,128)(2,1)S(1)} collective-permute-done((bf16[384,896]{1,0:T(8,128)(2,1)S(1)}, bf16[384,896]{1,0:T(8,128)(2,1)S(1)}, u32[]{:S(2)}, u32[]{:S(2)}) %collective-permute-start.4) | collective-permute-done | bytes 688160 | tf_op jit(solution)/shard_map/ppermute | solution.py:122
  92.5 5.0 %collective-permute-done.5 = bf16[512,896]{1,0:T(8,128)(2,1)S(1)} collective-permute-done((bf16[512,896]{1,0:T(8,128)(2,1)S(1)}, bf16[512,896]{1,0:T(8,128)(2,1)S(1)}, u32[]{:S(2)}, u32[]{:S(2)}) %collective-permute-start.5) | collective-permute-done | bytes 917536 | tf_op jit(solution)/shard_map/ppermute | solution.py:114
  97.6 2.6 convolution_convert_fusion.12
  105.4 2.6 convolution_convert_fusion.13
  108.0 5.0 %fusion.29 = bf16[512,896]{1,0:T(8,128)(2,1)S(1)} fusion(bf16[896,4096]{0,1:T(8,128)(2,1)S(1)} %convert_bitcast_fusion, s32[512]{0:T(512)S(1)} %pad_add_fusion.6), kind=kOutput, calls=%fused_computation.70 | convolution fusion | flops 3760652288 | bytes 8259584 | tf_op jit(solution)/shard_map/dot_general | solution.py:107
  114.0 10.7 %collective-permute-done.8 = bf16[512,896]{1,0:T(8,128)(2,1)S(1)} collective-permute-done((bf16[512,896]{1,0:T(8,128)(2,1)S(1)}, bf16[512,896]{1,0:T(8,128)(2,1)S(1)}, u32[]{:S(2)}, u32[]{:S(2)}) %collective-permute-start.8) | collective-permute-done | bytes 917536 | tf_op jit(solution)/shard_map/ppermute | solution.py:122
  126.1 2.6 collective-permute-done.6
  128.9 3.7 convolution_convert_fusion.8
  137.8 2.4 convolution_convert_fusion.9
  140.2 4.5 %fusion.28 = bf16[512,896]{1,0:T(8,128)(2,1)S(1)} fusion(bf16[896,4096]{0,1:T(8,128)(2,1)S(1)} %convert_bitcast_fusion, s32[512]{0:T(512)S(1)} %pad_add_fusion.7), kind=kOutput, calls=%fused_computation.69 | convolution fusion | flops 3760652288 | bytes 8259584 | tf_op jit(solution)/shard_map/dot_general | solution.py:107
  145.8 10.1 %collective-permute-done.11 = bf16[512,896]{1,0:T(8,128)(2,1)S(1)} collective-permute-done((bf16[512,896]{1,0:T(8,128)(2,1)S(1)}, bf16[512,896]{1,0:T(8,128)(2,1)S(1)}, u32[]{:S(2)}, u32[]{:S(2)}) %collective-permute-start.11) | collective-permute-done | bytes 917536 | tf_op jit(solution)/shard_map/ppermute | solution.py:122
  157.5 3.9 convolution_convert_fusion.6
  164.5 2.4 convolution_convert_fusion.7
  166.8 4.5 %fusion.27 = bf16[512,896]{1,0:T(8,128)(2,1)S(1)} fusion(bf16[896,4096]{0,1:T(8,128)(2,1)S(1)} %convert_bitcast_fusion, s32[512]{0:T(512)S(1)} %pad_add_fusion.8), kind=kOutput, calls=%fused_computation.68 | convolution fusion | flops 3760652288 | bytes 8259584 | tf_op jit(solution)/shard_map/dot_general | solution.py:107
  171.4 4.4 %collective-permute-start.22 = (bf16[192,4096]{1,0:T(8,128)(2,1)S(1)}, bf16[192,4096]{1,0:T(8,128)(2,1)S(1)}, u32[]{:S(2)}, u32[]{:S(2)}) collective-permute-start(bf16[192,4096]{1,0:T(8,128)(2,1)S(1)} %slice_add_fusion.4), channel_id=1, source_target_pairs={{0,2},{1,3},{2,0},{3,1},{4,6},{5,7},{6,4},{7,5},{8,10},{9,11},{10,... | collective-permute-start | bytes 4718600 | tf_op jit(solution)/shard_map/ppermute | solution.py:154
  176.1 9.1 %collective-permute-done.15 = bf16[512,896]{1,0:T(8,128)(2,1)S(1)} collective-permute-done((bf16[512,896]{1,0:T(8,128)(2,1)S(1)}, bf16[512,896]{1,0:T(8,128)(2,1)S(1)}, u32[]{:S(2)}, u32[]{:S(2)}) %collective-permute-start.15) | collective-permute-done | bytes 917536 | tf_op jit(solution)/shard_map/ppermute | solution.py:122
  188.4 3.7 convolution_convert_fusion.4
  197.1 2.4 convolution_convert_fusion.5
  199.5 4.3 fusion.32
  203.8 4.9 %collective-permute-start.27 = (bf16[192,4096]{1,0:T(8,128)(2,1)}, bf16[192,4096]{1,0:T(8,128)(2,1)S(1)}, u32[]{:S(2)}, u32[]{:S(2)}) collective-permute-start(bf16[192,4096]{1,0:T(8,128)(2,1)} %pad_maximum_fusion), channel_id=1, source_target_pairs={{0,2},{1,3},{2,0},{3,1},{4,6},{5,7},{6,4},{7,5},{8,10},{9,11},{10,... | collective-permute-start | bytes 4718600 | tf_op jit(solution)/shard_map/ppermute | solution.py:154
  209.7 5.4 %collective-permute-done.20 = bf16[512,896]{1,0:T(8,128)(2,1)S(1)} collective-permute-done((bf16[512,896]{1,0:T(8,128)(2,1)S(1)}, bf16[512,896]{1,0:T(8,128)(2,1)S(1)}, u32[]{:S(2)}, u32[]{:S(2)}) %collective-permute-start.20) | collective-permute-done | bytes 917536 | tf_op jit(solution)/shard_map/ppermute | solution.py:122
  218.8 3.7 convolution_convert_fusion.2
  227.4 2.4 convolution_convert_fusion.3
  229.8 3.2 fusion.35
  233.0 7.6 %collective-permute-start.32 = (bf16[192,4096]{1,0:T(8,128)(2,1)}, bf16[192,4096]{1,0:T(8,128)(2,1)S(1)}, u32[]{:S(2)}, u32[]{:S(2)}) collective-permute-start(bf16[192,4096]{1,0:T(8,128)(2,1)} %pad_maximum_fusion.1), channel_id=1, source_target_pairs={{0,2},{1,3},{2,0},{3,1},{4,6},{5,7},{6,4},{7,5},{8,10},{9,11},{10,... | collective-permute-start | bytes 4718600 | tf_op jit(solution)/shard_map/ppermute | solution.py:154
  241.7 3.9 collective-permute-done.25
  246.7 2.1 collective-permute-start.28
  249.1 3.7 convolution_convert_fusion
  256.5 2.0 fusion.36
  260.0 5.1 %convolution_convert_fusion.1 = bf16[256,4096]{1,0:T(8,128)(2,1)} fusion(bf16[896,4096]{0,1:T(8,128)(2,1)S(1)} %convert_bitcast_fusion, bf16[512,896]{1,0:T(8,128)(2,1)} %copy-done.18), kind=kOutput, calls=%fused_computation.24 | convolution fusion | flops 1880096768 | bytes 9895936 | tf_op jit(solution)/shard_map/dot_general | solution.py:131
  266.7 8.4 %collective-permute-start.37 = (bf16[192,4096]{1,0:T(8,128)(2,1)}, bf16[192,4096]{1,0:T(8,128)(2,1)S(1)}, u32[]{:S(2)}, u32[]{:S(2)}) collective-permute-start(bf16[192,4096]{1,0:T(8,128)(2,1)} %pad_maximum_fusion.2), channel_id=1, source_target_pairs={{0,2},{1,3},{2,0},{3,1},{4,6},{5,7},{6,4},{7,5},{8,10},{9,11},{10,... | collective-permute-start | bytes 4718600 | tf_op jit(solution)/shard_map/ppermute | solution.py:154
  276.7 1.9 slice_add_fusion.18
  280.1 1.8 collective-permute-start.33
  283.2 3.8 convolution_convert_fusion.10
  287.0 2.0 add.340
  293.6 2.6 convolution_convert_fusion.11
  297.9 3.9 collective-permute-start.41
  303.1 1.8 slice_add_fusion.25
  306.2 3.5 convolution_convert_fusion.16
  309.7 2.5 convolution_convert_fusion.17
  317.2 5.9 %collective-permute-start.44 = (bf16[144,4096]{1,0:T(8,128)(2,1)S(1)}, bf16[144,4096]{1,0:T(8,128)(2,1)S(1)}, u32[]{:S(2)}, u32[]{:S(2)}) collective-permute-start(bf16[144,4096]{1,0:T(8,128)(2,1)S(1)} %pad_maximum_fusion.4), channel_id=1, source_target_pairs={{0,2},{1,3},{2,0},{3,1},{4,6},{5,7},{6,4},{7,5},{8,10},{9,11},{10,... | collective-permute-start | bytes 3538952 | tf_op jit(solution)/shard_map/ppermute | solution.py:154
  324.9 20.4 %collective-permute-done.41 = bf16[192,4096]{1,0:T(8,128)(2,1)S(1)} collective-permute-done((bf16[192,4096]{1,0:T(8,128)(2,1)}, bf16[192,4096]{1,0:T(8,128)(2,1)S(1)}, u32[]{:S(2)}, u32[]{:S(2)}) %collective-permute-start.41) | collective-permute-done | bytes 1572896 | tf_op jit(solution)/shard_map/ppermute | solution.py:154
  346.3 1.8 collective-permute-start.42
  348.2 3.2 convolution_convert_fusion.18
  351.6 4.0 collective-permute-start.47
  357.3 2.4 convolution_convert_fusion.19
  364.1 6.4 %collective-permute-done.44 = bf16[144,4096]{1,0:T(8,128)(2,1)S(1)} collective-permute-done((bf16[144,4096]{1,0:T(8,128)(2,1)S(1)}, bf16[144,4096]{1,0:T(8,128)(2,1)S(1)}, u32[]{:S(2)}, u32[]{:S(2)}) %collective-permute-start.44) | collective-permute-done | bytes 1179680 | tf_op jit(solution)/shard_map/ppermute | solution.py:154
  371.3 10.4 %collective-permute-start.51 = (bf16[48,4096]{1,0:T(8,128)(2,1)S(1)}, bf16[48,4096]{1,0:T(8,128)(2,1)S(1)}, u32[]{:S(2)}, u32[]{:S(2)}) collective-permute-start(bf16[48,4096]{1,0:T(8,128)(2,1)S(1)} %slice_add_fusion.24), channel_id=1, source_target_pairs={{0,2},{1,3},{6,4},{7,5},{8,10},{9,11},{14,12},{15,13},{16,18},{17,... | collective-permute-start | bytes 1179656 | tf_op jit(solution)/shard_map/ppermute | solution.py:154
  381.7 1.8 subtract_dynamic-update-slice_fusion.1
  383.5 14.7 %collective-permute-done.45 = bf16[64,4096]{1,0:T(8,128)(2,1)S(1)} collective-permute-done((bf16[64,4096]{1,0:T(8,128)(2,1)S(1)}, bf16[64,4096]{1,0:T(8,128)(2,1)S(1)}, u32[]{:S(2)}, u32[]{:S(2)}) %collective-permute-start.45) | collective-permute-done | bytes 524320 | tf_op jit(solution)/shard_map/ppermute | solution.py:174
  402.8 8.2 %collective-permute-done.48 = bf16[48,4096]{1,0:T(8,128)(2,1)S(1)} collective-permute-done((bf16[48,4096]{1,0:T(8,128)(2,1)S(1)}, bf16[48,4096]{1,0:T(8,128)(2,1)S(1)}, u32[]{:S(2)}, u32[]{:S(2)}) %collective-permute-start.48) | collective-permute-done | bytes 393248 | tf_op jit(solution)/shard_map/ppermute | solution.py:174
  413.5 10.4 %collective-permute-done.50 = bf16[32,4096]{1,0:T(8,128)(2,1)S(1)} collective-permute-done((bf16[32,4096]{1,0:T(8,128)(2,1)S(1)}, bf16[32,4096]{1,0:T(8,128)(2,1)S(1)}, u32[]{:S(2)}, u32[]{:S(2)}) %collective-permute-start.50) | collective-permute-done | bytes 262176 | tf_op jit(solution)/shard_map/ppermute | solution.py:174
  425.6 6.3 %collective-permute-done.53 = bf16[16,4096]{1,0:T(8,128)(2,1)S(1)} collective-permute-done((bf16[16,4096]{1,0:T(8,128)(2,1)S(1)}, bf16[16,4096]{1,0:T(8,128)(2,1)S(1)}, u32[]{:S(2)}, u32[]{:S(2)}) %collective-permute-start.53) | collective-permute-done | bytes 131104 | tf_op jit(solution)/shard_map/ppermute | solution.py:174
  (281 shorter events, 99.0 us)
Async XLA Ops:
  0.0 25.9 %copy-start = (bf16[896,896]{1,0:T(8,128)(2,1)S(1)}, bf16[896,896]{1,0:T(8,128)(2,1)}, u32[]{:S(2)}) copy-start(bf16[896,896]{1,0:T(8,128)(2,1)} %param.15) | copy-start | bytes 4816900
  2.1 9.8 %all-to-all-start = ((f32[4,2,128]{2,1,0:T(2,128)}), f32[4,2,128]{2,1,0:T(2,128)S(1)}, u32[]{:S(2)}, u32[]{:S(2)}) async-start(f32[4,2,128]{2,1,0:T(2,128)} %pad_maximum_fusion.6), calls=%async_computation | async-start | bytes 8192 | tf_op jit(solution)/shard_map/all_to_all | solution.py:27
  38.5 15.8 %collective-permute-start = (bf16[384,896]{1,0:T(8,128)(2,1)S(1)}, bf16[384,896]{1,0:T(8,128)(2,1)S(1)}, u32[]{:S(2)}, u32[]{:S(2)}) collective-permute-start(bf16[384,896]{1,0:T(8,128)(2,1)S(1)} %fusion.34), channel_id=1, source_target_pairs={{0,8},{8,0},{16,24},{24,16},{1,9},{9,1},{17,25},{25,17},{2,10},{10... | collective-permute-start | bytes 2064392 | tf_op jit(solution)/shard_map/ppermute | solution.py:114
  54.5 15.4 %collective-permute-start.1 = (bf16[384,896]{1,0:T(8,128)(2,1)S(1)}, bf16[384,896]{1,0:T(8,128)(2,1)S(1)}, u32[]{:S(2)}, u32[]{:S(2)}) collective-permute-start(bf16[384,896]{1,0:T(8,128)(2,1)S(1)} %add.297), channel_id=1, source_target_pairs={{0,16},{8,24},{16,0},{24,8},{1,17},{9,25},{17,1},{25,9},{2,18},{10... | collective-permute-start | bytes 2064392 | tf_op jit(solution)/shard_map/ppermute | solution.py:122
  56.0 15.4 %collective-permute-start.2 = (bf16[384,896]{1,0:T(8,128)(2,1)S(1)}, bf16[384,896]{1,0:T(8,128)(2,1)S(1)}, u32[]{:S(2)}, u32[]{:S(2)}) collective-permute-start(bf16[384,896]{1,0:T(8,128)(2,1)S(1)} %fusion.33), channel_id=1, source_target_pairs={{0,8},{8,0},{16,24},{24,16},{1,9},{9,1},{17,25},{25,17},{2,10},{10... | collective-permute-start | bytes 2064392 | tf_op jit(solution)/shard_map/ppermute | solution.py:114
  74.3 9.5 %collective-permute-start.3 = (bf16[192,4096]{1,0:T(8,128)(2,1)S(1)}, bf16[192,4096]{1,0:T(8,128)(2,1)S(1)}, u32[]{:S(2)}, u32[]{:S(2)}) collective-permute-start(bf16[192,4096]{1,0:T(8,128)(2,1)S(1)} %convolution_convert_fusion.14), channel_id=1, source_target_pairs={{0,1},{1,0},{2,3},{3,2},{4,5},{5,4},{6,7},{7,6},{8,9},{9,8},{10,11... | collective-permute-start | bytes 4718600 | tf_op jit(solution)/shard_map/ppermute | solution.py:135
  74.6 17.9 %collective-permute-start.4 = (bf16[384,896]{1,0:T(8,128)(2,1)S(1)}, bf16[384,896]{1,0:T(8,128)(2,1)S(1)}, u32[]{:S(2)}, u32[]{:S(2)}) collective-permute-start(bf16[384,896]{1,0:T(8,128)(2,1)S(1)} %add.301), channel_id=1, source_target_pairs={{0,16},{8,24},{16,0},{24,8},{1,17},{9,25},{17,1},{25,9},{2,18},{10... | collective-permute-start | bytes 2064392 | tf_op jit(solution)/shard_map/ppermute | solution.py:122
  75.0 22.5 %collective-permute-start.5 = (bf16[512,896]{1,0:T(8,128)(2,1)S(1)}, bf16[512,896]{1,0:T(8,128)(2,1)S(1)}, u32[]{:S(2)}, u32[]{:S(2)}) collective-permute-start(bf16[512,896]{1,0:T(8,128)(2,1)S(1)} %fusion.31), channel_id=1, source_target_pairs={{0,8},{8,0},{16,24},{24,16},{1,9},{9,1},{17,25},{25,17},{2,10},{10... | collective-permute-start | bytes 2752520 | tf_op jit(solution)/shard_map/ppermute | solution.py:114
  100.2 12.8 %collective-permute-start.7 = (bf16[192,4096]{1,0:T(8,128)(2,1)S(1)}, bf16[192,4096]{1,0:T(8,128)(2,1)S(1)}, u32[]{:S(2)}, u32[]{:S(2)}) collective-permute-start(bf16[192,4096]{1,0:T(8,128)(2,1)S(1)} %convolution_convert_fusion.12), channel_id=1, source_target_pairs={{0,1},{1,0},{2,3},{3,2},{4,5},{5,4},{6,7},{7,6},{8,9},{9,8},{10,11... | collective-permute-start | bytes 4718600 | tf_op jit(solution)/shard_map/ppermute | solution.py:135
  100.3 28.4 %collective-permute-start.6 = (bf16[144,4096]{1,0:T(8,128)(2,1)S(1)}, bf16[144,4096]{1,0:T(8,128)(2,1)S(1)}, u32[]{:S(2)}, u32[]{:S(2)}) collective-permute-start(bf16[144,4096]{1,0:T(8,128)(2,1)S(1)} %slice_add_fusion.7), channel_id=1, source_target_pairs={{0,2},{1,3},{2,0},{3,1},{4,6},{5,7},{6,4},{7,5},{8,10},{9,11},{10,... | collective-permute-start | bytes 3538952 | tf_op jit(solution)/shard_map/ppermute | solution.py:154
  102.2 22.5 %collective-permute-start.8 = (bf16[512,896]{1,0:T(8,128)(2,1)S(1)}, bf16[512,896]{1,0:T(8,128)(2,1)S(1)}, u32[]{:S(2)}, u32[]{:S(2)}) collective-permute-start(bf16[512,896]{1,0:T(8,128)(2,1)S(1)} %add.305), channel_id=1, source_target_pairs={{0,16},{8,24},{16,0},{24,8},{1,17},{9,25},{17,1},{25,9},{2,18},{10... | collective-permute-start | bytes 2752520 | tf_op jit(solution)/shard_map/ppermute | solution.py:122
  103.9 22.1 %collective-permute-start.9 = (bf16[512,896]{1,0:T(8,128)(2,1)S(1)}, bf16[512,896]{1,0:T(8,128)(2,1)S(1)}, u32[]{:S(2)}, u32[]{:S(2)}) collective-permute-start(bf16[512,896]{1,0:T(8,128)(2,1)S(1)} %fusion.30), channel_id=1, source_target_pairs={{0,8},{8,0},{16,24},{24,16},{1,9},{9,1},{17,25},{25,17},{2,10},{10... | collective-permute-start | bytes 2752520 | tf_op jit(solution)/shard_map/ppermute | solution.py:114
  128.7 32.6 %copy-start.12 = (bf16[144,4096]{1,0:T(8,128)(2,1)}, bf16[144,4096]{1,0:T(8,128)(2,1)S(1)}, u32[]{:S(2)}) copy-start(bf16[144,4096]{1,0:T(8,128)(2,1)S(1)} %collective-permute-done.6) | copy-start | bytes 3538948
  132.6 12.1 %collective-permute-start.10 = (bf16[256,4096]{1,0:T(8,128)(2,1)}, bf16[256,4096]{1,0:T(8,128)(2,1)S(1)}, u32[]{:S(2)}, u32[]{:S(2)}) collective-permute-start(bf16[256,4096]{1,0:T(8,128)(2,1)} %convolution_convert_fusion.8), channel_id=1, source_target_pairs={{0,1},{1,0},{2,3},{3,2},{4,5},{5,4},{6,7},{7,6},{8,9},{9,8},{10,11... | collective-permute-start | bytes 6291464 | tf_op jit(solution)/shard_map/ppermute | solution.py:135
  133.0 22.8 %collective-permute-start.11 = (bf16[512,896]{1,0:T(8,128)(2,1)S(1)}, bf16[512,896]{1,0:T(8,128)(2,1)S(1)}, u32[]{:S(2)}, u32[]{:S(2)}) collective-permute-start(bf16[512,896]{1,0:T(8,128)(2,1)S(1)} %add.309), channel_id=1, source_target_pairs={{0,16},{8,24},{16,0},{24,8},{1,17},{9,25},{17,1},{25,9},{2,18},{10... | collective-permute-start | bytes 2752520 | tf_op jit(solution)/shard_map/ppermute | solution.py:122
  134.8 22.5 %collective-permute-start.12 = (bf16[512,896]{1,0:T(8,128)(2,1)S(1)}, bf16[512,896]{1,0:T(8,128)(2,1)S(1)}, u32[]{:S(2)}, u32[]{:S(2)}) collective-permute-start(bf16[512,896]{1,0:T(8,128)(2,1)S(1)} %fusion.29), channel_id=1, source_target_pairs={{0,8},{8,0},{16,24},{24,16},{1,9},{9,1},{17,25},{25,17},{2,10},{10... | collective-permute-start | bytes 2752520 | tf_op jit(solution)/shard_map/ppermute | solution.py:114
  136.2 49.0 %collective-permute-start.17 = (bf16[144,4096]{1,0:T(8,128)(2,1)S(1)}, bf16[144,4096]{1,0:T(8,128)(2,1)S(1)}, u32[]{:S(2)}, u32[]{:S(2)}) collective-permute-start(bf16[144,4096]{1,0:T(8,128)(2,1)S(1)} %slice_add_fusion.6), channel_id=1, source_target_pairs={{0,2},{1,3},{2,0},{3,1},{4,6},{5,7},{6,4},{7,5},{8,10},{9,11},{10,... | collective-permute-start | bytes 3538952 | tf_op jit(solution)/shard_map/ppermute | solution.py:154
  161.3 10.0 %collective-permute-start.14 = (bf16[256,4096]{1,0:T(8,128)(2,1)}, bf16[256,4096]{1,0:T(8,128)(2,1)S(1)}, u32[]{:S(2)}, u32[]{:S(2)}) collective-permute-start(bf16[256,4096]{1,0:T(8,128)(2,1)} %convolution_convert_fusion.6), channel_id=1, source_target_pairs={{0,1},{1,0},{2,3},{3,2},{4,5},{5,4},{6,7},{7,6},{8,9},{9,8},{10,11... | collective-permute-start | bytes 6291464 | tf_op jit(solution)/shard_map/ppermute | solution.py:135
  161.4 14.6 %collective-permute-start.13 = (bf16[96,4096]{1,0:T(8,128)(2,1)S(1)}, bf16[96,4096]{1,0:T(8,128)(2,1)S(1)}, u32[]{:S(2)}, u32[]{:S(2)}) collective-permute-start(bf16[96,4096]{1,0:T(8,128)(2,1)S(1)} %slice_add_fusion.16), channel_id=1, source_target_pairs={{2,4},{3,5},{4,2},{5,3},{10,12},{11,13},{12,10},{13,11},{18,20},{1... | collective-permute-start | bytes 2359304 | tf_op jit(solution)/shard_map/ppermute | solution.py:169
  162.4 22.8 %collective-permute-start.15 = (bf16[512,896]{1,0:T(8,128)(2,1)S(1)}, bf16[512,896]{1,0:T(8,128)(2,1)S(1)}, u32[]{:S(2)}, u32[]{:S(2)}) collective-permute-start(bf16[512,896]{1,0:T(8,128)(2,1)S(1)} %add.314), channel_id=1, source_target_pairs={{0,16},{8,24},{16,0},{24,8},{1,17},{9,25},{17,1},{25,9},{2,18},{10... | collective-permute-start | bytes 2752520 | tf_op jit(solution)/shard_map/ppermute | solution.py:122
  162.8 22.5 %collective-permute-start.16 = (bf16[512,896]{1,0:T(8,128)(2,1)S(1)}, bf16[512,896]{1,0:T(8,128)(2,1)S(1)}, u32[]{:S(2)}, u32[]{:S(2)}) collective-permute-start(bf16[512,896]{1,0:T(8,128)(2,1)S(1)} %fusion.28), channel_id=1, source_target_pairs={{0,8},{8,0},{16,24},{24,16},{1,9},{9,1},{17,25},{25,17},{2,10},{10... | collective-permute-start | bytes 2752520 | tf_op jit(solution)/shard_map/ppermute | solution.py:114
  171.4 45.2 %collective-permute-start.22 = (bf16[192,4096]{1,0:T(8,128)(2,1)S(1)}, bf16[192,4096]{1,0:T(8,128)(2,1)S(1)}, u32[]{:S(2)}, u32[]{:S(2)}) collective-permute-start(bf16[192,4096]{1,0:T(8,128)(2,1)S(1)} %slice_add_fusion.4), channel_id=1, source_target_pairs={{0,2},{1,3},{2,0},{3,1},{4,6},{5,7},{6,4},{7,5},{8,10},{9,11},{10,... | collective-permute-start | bytes 4718600 | tf_op jit(solution)/shard_map/ppermute | solution.py:154
  176.0 19.6 %copy-start.21 = (bf16[96,4096]{1,0:T(8,128)(2,1)}, bf16[96,4096]{1,0:T(8,128)(2,1)S(1)}, u32[]{:S(2)}) copy-start(bf16[96,4096]{1,0:T(8,128)(2,1)S(1)} %collective-permute-done.13) | copy-start | bytes 2359300
  186.4 23.3 %collective-permute-start.18 = (bf16[96,4096]{1,0:T(8,128)(2,1)}, bf16[96,4096]{1,0:T(8,128)(2,1)}, u32[]{:S(2)}, u32[]{:S(2)}) collective-permute-start(bf16[96,4096]{1,0:T(8,128)(2,1)} %slice_add_fusion.15), channel_id=1, source_target_pairs={{2,4},{3,5},{4,2},{5,3},{10,12},{11,13},{12,10},{13,11},{18,20},{1... | collective-permute-start | bytes 2359304 | tf_op jit(solution)/shard_map/ppermute | solution.py:169
  192.1 11.7 %collective-permute-start.19 = (bf16[256,4096]{1,0:T(8,128)(2,1)}, bf16[256,4096]{1,0:T(8,128)(2,1)S(1)}, u32[]{:S(2)}, u32[]{:S(2)}) collective-permute-start(bf16[256,4096]{1,0:T(8,128)(2,1)} %convolution_convert_fusion.4), channel_id=1, source_target_pairs={{0,1},{1,0},{2,3},{3,2},{4,5},{5,4},{6,7},{7,6},{8,9},{9,8},{10,11... | collective-permute-start | bytes 6291464 | tf_op jit(solution)/shard_map/ppermute | solution.py:135
  192.3 22.8 %collective-permute-start.20 = (bf16[512,896]{1,0:T(8,128)(2,1)S(1)}, bf16[512,896]{1,0:T(8,128)(2,1)S(1)}, u32[]{:S(2)}, u32[]{:S(2)}) collective-permute-start(bf16[512,896]{1,0:T(8,128)(2,1)S(1)} %add.319), channel_id=1, source_target_pairs={{0,16},{8,24},{16,0},{24,8},{1,17},{9,25},{17,1},{25,9},{2,18},{10... | collective-permute-start | bytes 2752520 | tf_op jit(solution)/shard_map/ppermute | solution.py:122
  194.1 22.5 %collective-permute-start.21 = (bf16[512,896]{1,0:T(8,128)(2,1)S(1)}, bf16[512,896]{1,0:T(8,128)(2,1)S(1)}, u32[]{:S(2)}, u32[]{:S(2)}) collective-permute-start(bf16[512,896]{1,0:T(8,128)(2,1)S(1)} %fusion.27), channel_id=1, source_target_pairs={{0,8},{8,0},{16,24},{24,16},{1,9},{9,1},{17,25},{25,17},{2,10},{10... | collective-permute-start | bytes 2752520 | tf_op jit(solution)/shard_map/ppermute | solution.py:114
  203.8 41.7 %collective-permute-start.27 = (bf16[192,4096]{1,0:T(8,128)(2,1)}, bf16[192,4096]{1,0:T(8,128)(2,1)S(1)}, u32[]{:S(2)}, u32[]{:S(2)}) collective-permute-start(bf16[192,4096]{1,0:T(8,128)(2,1)} %pad_maximum_fusion), channel_id=1, source_target_pairs={{0,2},{1,3},{2,0},{3,1},{4,6},{5,7},{6,4},{7,5},{8,10},{9,11},{10,... | collective-permute-start | bytes 4718600 | tf_op jit(solution)/shard_map/ppermute | solution.py:154
  216.7 28.9 %collective-permute-start.23 = (bf16[128,4096]{1,0:T(8,128)(2,1)S(1)}, bf16[128,4096]{1,0:T(8,128)(2,1)S(1)}, u32[]{:S(2)}, u32[]{:S(2)}) collective-permute-start(bf16[128,4096]{1,0:T(8,128)(2,1)S(1)} %slice_add_fusion.12), channel_id=1, source_target_pairs={{2,4},{3,5},{4,2},{5,3},{10,12},{11,13},{12,10},{13,11},{18,20},{1... | collective-permute-start | bytes 3145736 | tf_op jit(solution)/shard_map/ppermute | solution.py:169
  222.5 10.5 %collective-permute-start.24 = (bf16[256,4096]{1,0:T(8,128)(2,1)}, bf16[256,4096]{1,0:T(8,128)(2,1)S(1)}, u32[]{:S(2)}, u32[]{:S(2)}) collective-permute-start(bf16[256,4096]{1,0:T(8,128)(2,1)} %convolution_convert_fusion.2), channel_id=1, source_target_pairs={{0,1},{1,0},{2,3},{3,2},{4,5},{5,4},{6,7},{7,6},{8,9},{9,8},{10,11... | collective-permute-start | bytes 6291464 | tf_op jit(solution)/shard_map/ppermute | solution.py:135
  222.7 22.8 %collective-permute-start.25 = (bf16[512,896]{1,0:T(8,128)(2,1)S(1)}, bf16[512,896]{1,0:T(8,128)(2,1)S(1)}, u32[]{:S(2)}, u32[]{:S(2)}) collective-permute-start(bf16[512,896]{1,0:T(8,128)(2,1)S(1)} %add.324), channel_id=1, source_target_pairs={{0,16},{8,24},{16,0},{24,8},{1,17},{9,25},{17,1},{25,9},{2,18},{10... | collective-permute-start | bytes 2752520 | tf_op jit(solution)/shard_map/ppermute | solution.py:122
  223.2 18.5 %collective-permute-start.26 = (bf16[384,896]{1,0:T(8,128)(2,1)}, bf16[384,896]{1,0:T(8,128)(2,1)}, u32[]{:S(2)}, u32[]{:S(2)}) collective-permute-start(bf16[384,896]{1,0:T(8,128)(2,1)} %fusion.32), channel_id=1, source_target_pairs={{0,8},{8,0},{16,24},{24,16},{1,9},{9,1},{17,25},{25,17},{2,10},{10... | collective-permute-start | bytes 2064392 | tf_op jit(solution)/shard_map/ppermute | solution.py:114
  233.0 45.6 %collective-permute-start.32 = (bf16[192,4096]{1,0:T(8,128)(2,1)}, bf16[192,4096]{1,0:T(8,128)(2,1)S(1)}, u32[]{:S(2)}, u32[]{:S(2)}) collective-permute-start(bf16[192,4096]{1,0:T(8,128)(2,1)} %pad_maximum_fusion.1), channel_id=1, source_target_pairs={{0,2},{1,3},{2,0},{3,1},{4,6},{5,7},{6,4},{7,5},{8,10},{9,11},{10,... | collective-permute-start | bytes 4718600 | tf_op jit(solution)/shard_map/ppermute | solution.py:154
  245.6 10.8 %copy-start.14 = (bf16[128,4096]{1,0:T(8,128)(2,1)}, bf16[128,4096]{1,0:T(8,128)(2,1)S(1)}, u32[]{:S(2)}) copy-start(bf16[128,4096]{1,0:T(8,128)(2,1)S(1)} %collective-permute-done.23) | copy-start | bytes 3145732
  246.7 31.9 %collective-permute-start.28 = (bf16[128,4096]{1,0:T(8,128)(2,1)}, bf16[128,4096]{1,0:T(8,128)(2,1)}, u32[]{:S(2)}, u32[]{:S(2)}) collective-permute-start(bf16[128,4096]{1,0:T(8,128)(2,1)} %slice_add_fusion.11), channel_id=1, source_target_pairs={{2,4},{3,5},{4,2},{5,3},{10,12},{11,13},{12,10},{13,11},{18,20},{1... | collective-permute-start | bytes 3145736 | tf_op jit(solution)/shard_map/ppermute | solution.py:169
  252.8 13.9 %collective-permute-start.29 = (bf16[256,4096]{1,0:T(8,128)(2,1)}, bf16[256,4096]{1,0:T(8,128)(2,1)}, u32[]{:S(2)}, u32[]{:S(2)}) collective-permute-start(bf16[256,4096]{1,0:T(8,128)(2,1)} %convolution_convert_fusion), channel_id=1, source_target_pairs={{0,1},{1,0},{2,3},{3,2},{4,5},{5,4},{6,7},{7,6},{8,9},{9,8},{10,11... | collective-permute-start | bytes 6291464 | tf_op jit(solution)/shard_map/ppermute | solution.py:135
  254.3 24.3 %collective-permute-start.30 = (bf16[384,896]{1,0:T(8,128)(2,1)S(1)}, bf16[384,896]{1,0:T(8,128)(2,1)}, u32[]{:S(2)}, u32[]{:S(2)}) collective-permute-start(bf16[384,896]{1,0:T(8,128)(2,1)S(1)} %add.332), channel_id=1, source_target_pairs={{0,16},{8,24},{16,0},{24,8},{1,17},{9,25},{17,1},{25,9},{2,18},{10... | collective-permute-start | bytes 2064392 | tf_op jit(solution)/shard_map/ppermute | solution.py:122
  255.0 23.7 %collective-permute-start.31 = (bf16[256,896]{1,0:T(8,128)(2,1)}, bf16[256,896]{1,0:T(8,128)(2,1)}, u32[]{:S(2)}, u32[]{:S(2)}) collective-permute-start(bf16[256,896]{1,0:T(8,128)(2,1)} %fusion.35), channel_id=1, source_target_pairs={{0,8},{8,0},{16,24},{24,16},{1,9},{9,1},{17,25},{25,17},{2,10},{10... | collective-permute-start | bytes 1376264 | tf_op jit(solution)/shard_map/ppermute | solution.py:114
  266.7 45.4 %collective-permute-start.37 = (bf16[192,4096]{1,0:T(8,128)(2,1)}, bf16[192,4096]{1,0:T(8,128)(2,1)S(1)}, u32[]{:S(2)}, u32[]{:S(2)}) collective-permute-start(bf16[192,4096]{1,0:T(8,128)(2,1)} %pad_maximum_fusion.2), channel_id=1, source_target_pairs={{0,2},{1,3},{2,0},{3,1},{4,6},{5,7},{6,4},{7,5},{8,10},{9,11},{10,... | collective-permute-start | bytes 4718600 | tf_op jit(solution)/shard_map/ppermute | solution.py:154
  280.1 24.8 %collective-permute-start.33 = (bf16[128,4096]{1,0:T(8,128)(2,1)}, bf16[128,4096]{1,0:T(8,128)(2,1)}, u32[]{:S(2)}, u32[]{:S(2)}) collective-permute-start(bf16[128,4096]{1,0:T(8,128)(2,1)} %slice_add_fusion.10), channel_id=1, source_target_pairs={{2,4},{3,5},{4,2},{5,3},{10,12},{11,13},{12,10},{13,11},{18,20},{1... | collective-permute-start | bytes 3145736 | tf_op jit(solution)/shard_map/ppermute | solution.py:169
  287.0 10.8 %collective-permute-start.34 = (bf16[192,4096]{1,0:T(8,128)(2,1)}, bf16[192,4096]{1,0:T(8,128)(2,1)}, u32[]{:S(2)}, u32[]{:S(2)}) collective-permute-start(bf16[192,4096]{1,0:T(8,128)(2,1)} %convolution_convert_fusion.10), channel_id=1, source_target_pairs={{0,1},{1,0},{2,3},{3,2},{4,5},{5,4},{6,7},{7,6},{8,9},{9,8},{10,11... | collective-permute-start | bytes 4718600 | tf_op jit(solution)/shard_map/ppermute | solution.py:135
  289.1 15.9 %collective-permute-start.35 = (bf16[256,896]{1,0:T(8,128)(2,1)}, bf16[256,896]{1,0:T(8,128)(2,1)}, u32[]{:S(2)}, u32[]{:S(2)}) collective-permute-start(bf16[256,896]{1,0:T(8,128)(2,1)} %add.340), channel_id=1, source_target_pairs={{0,16},{8,24},{16,0},{24,8},{1,17},{9,25},{17,1},{25,9},{2,18},{10... | collective-permute-start | bytes 1376264 | tf_op jit(solution)/shard_map/ppermute | solution.py:122
  290.5 14.4 %collective-permute-start.36 = (bf16[128,896]{1,0:T(8,128)(2,1)}, bf16[128,896]{1,0:T(8,128)(2,1)}, u32[]{:S(2)}, u32[]{:S(2)}) collective-permute-start(bf16[128,896]{1,0:T(8,128)(2,1)} %fusion.36), channel_id=1, source_target_pairs={{0,8},{8,0},{16,24},{24,16},{1,9},{9,1},{17,25},{25,17},{2,10},{10... | collective-permute-start | bytes 688136 | tf_op jit(solution)/shard_map/ppermute | solution.py:114
  297.9 47.4 %collective-permute-start.41 = (bf16[192,4096]{1,0:T(8,128)(2,1)}, bf16[192,4096]{1,0:T(8,128)(2,1)S(1)}, u32[]{:S(2)}, u32[]{:S(2)}) collective-permute-start(bf16[192,4096]{1,0:T(8,128)(2,1)} %pad_maximum_fusion.3), channel_id=1, source_target_pairs={{0,2},{1,3},{2,0},{3,1},{4,6},{5,7},{6,4},{7,5},{8,10},{9,11},{10,... | collective-permute-start | bytes 4718600 | tf_op jit(solution)/shard_map/ppermute | solution.py:154
  312.3 12.6 %collective-permute-start.38 = (bf16[128,4096]{1,0:T(8,128)(2,1)S(1)}, bf16[128,4096]{1,0:T(8,128)(2,1)S(1)}, u32[]{:S(2)}, u32[]{:S(2)}) collective-permute-start(bf16[128,4096]{1,0:T(8,128)(2,1)S(1)} %slice_add_fusion.9), channel_id=1, source_target_pairs={{2,4},{3,5},{4,2},{5,3},{10,12},{11,13},{12,10},{13,11},{18,20},{1... | collective-permute-start | bytes 3145736 | tf_op jit(solution)/shard_map/ppermute | solution.py:169
  313.0 11.7 %collective-permute-start.39 = (bf16[128,4096]{1,0:T(8,128)(2,1)}, bf16[128,4096]{1,0:T(8,128)(2,1)S(1)}, u32[]{:S(2)}, u32[]{:S(2)}) collective-permute-start(bf16[128,4096]{1,0:T(8,128)(2,1)} %convolution_convert_fusion.16), channel_id=1, source_target_pairs={{0,1},{1,0},{2,3},{3,2},{4,5},{5,4},{6,7},{7,6},{8,9},{9,8},{10,11... | collective-permute-start | bytes 3145736 | tf_op jit(solution)/shard_map/ppermute | solution.py:135
  314.2 10.6 %collective-permute-start.40 = (bf16[128,896]{1,0:T(8,128)(2,1)S(1)}, bf16[128,896]{1,0:T(8,128)(2,1)S(1)}, u32[]{:S(2)}, u32[]{:S(2)}) collective-permute-start(bf16[128,896]{1,0:T(8,128)(2,1)S(1)} %add.348), channel_id=1, source_target_pairs={{0,16},{8,24},{16,0},{24,8},{1,17},{9,25},{17,1},{25,9},{2,18},{10... | collective-permute-start | bytes 688136 | tf_op jit(solution)/shard_map/ppermute | solution.py:122
  317.2 53.3 %collective-permute-start.44 = (bf16[144,4096]{1,0:T(8,128)(2,1)S(1)}, bf16[144,4096]{1,0:T(8,128)(2,1)S(1)}, u32[]{:S(2)}, u32[]{:S(2)}) collective-permute-start(bf16[144,4096]{1,0:T(8,128)(2,1)S(1)} %pad_maximum_fusion.4), channel_id=1, source_target_pairs={{0,2},{1,3},{2,0},{3,1},{4,6},{5,7},{6,4},{7,5},{8,10},{9,11},{10,... | collective-permute-start | bytes 3538952 | tf_op jit(solution)/shard_map/ppermute | solution.py:154
  324.9 20.4 %copy-start.16 = (bf16[128,4096]{1,0:T(8,128)(2,1)}, bf16[128,4096]{1,0:T(8,128)(2,1)S(1)}, u32[]{:S(2)}) copy-start(bf16[128,4096]{1,0:T(8,128)(2,1)S(1)} %collective-permute-done.38) | copy-start | bytes 3145732
  346.3 15.4 %collective-permute-start.42 = (bf16[128,4096]{1,0:T(8,128)(2,1)}, bf16[128,4096]{1,0:T(8,128)(2,1)}, u32[]{:S(2)}, u32[]{:S(2)}) collective-permute-start(bf16[128,4096]{1,0:T(8,128)(2,1)} %slice_add_fusion.8), channel_id=1, source_target_pairs={{2,4},{3,5},{4,2},{5,3},{10,12},{11,13},{12,10},{13,11},{18,20},{1... | collective-permute-start | bytes 3145736 | tf_op jit(solution)/shard_map/ppermute | solution.py:169
  351.4 8.2 %collective-permute-start.43 = (bf16[64,4096]{1,0:T(8,128)(2,1)}, bf16[64,4096]{1,0:T(8,128)(2,1)}, u32[]{:S(2)}, u32[]{:S(2)}) collective-permute-start(bf16[64,4096]{1,0:T(8,128)(2,1)} %convolution_convert_fusion.18), channel_id=1, source_target_pairs={{0,1},{1,0},{2,3},{3,2},{4,5},{5,4},{6,7},{7,6},{8,9},{9,8},{10,11... | collective-permute-start | bytes 1572872 | tf_op jit(solution)/shard_map/ppermute | solution.py:135
  351.6 48.0 %collective-permute-start.47 = (bf16[96,4096]{1,0:T(8,128)(2,1)S(1)}, bf16[96,4096]{1,0:T(8,128)(2,1)S(1)}, u32[]{:S(2)}, u32[]{:S(2)}) collective-permute-start(bf16[96,4096]{1,0:T(8,128)(2,1)S(1)} %pad_maximum_fusion.5), channel_id=1, source_target_pairs={{0,2},{1,3},{2,0},{3,1},{4,6},{5,7},{6,4},{7,5},{8,10},{9,11},{10,... | collective-permute-start | bytes 2359304 | tf_op jit(solution)/shard_map/ppermute | solution.py:154
  360.7 21.0 %copy-start.5 = (bf16[64,4096]{1,0:T(8,128)(2,1)S(1)}, bf16[64,4096]{1,0:T(8,128)(2,1)}, u32[]{:S(2)}) copy-start(bf16[64,4096]{1,0:T(8,128)(2,1)} %slice_add_fusion.20) | copy-start | bytes 1572868
  362.8 35.4 %collective-permute-start.45 = (bf16[64,4096]{1,0:T(8,128)(2,1)S(1)}, bf16[64,4096]{1,0:T(8,128)(2,1)S(1)}, u32[]{:S(2)}, u32[]{:S(2)}) collective-permute-start(bf16[64,4096]{1,0:T(8,128)(2,1)S(1)} %slice_add_fusion.23), channel_id=1, source_target_pairs={{2,0},{3,1},{4,6},{5,7},{10,8},{11,9},{12,14},{13,15},{18,16},{19,... | collective-permute-start | bytes 1572872 | tf_op jit(solution)/shard_map/ppermute | solution.py:174
  370.6 27.6 %collective-permute-start.46 = (bf16[96,4096]{1,0:T(8,128)(2,1)S(1)}, bf16[96,4096]{1,0:T(8,128)(2,1)S(1)}, u32[]{:S(2)}, u32[]{:S(2)}) collective-permute-start(bf16[96,4096]{1,0:T(8,128)(2,1)S(1)} %slice_add_fusion.13), channel_id=1, source_target_pairs={{2,4},{3,5},{4,2},{5,3},{10,12},{11,13},{12,10},{13,11},{18,20},{1... | collective-permute-start | bytes 2359304 | tf_op jit(solution)/shard_map/ppermute | solution.py:169
  371.3 40.9 %collective-permute-start.51 = (bf16[48,4096]{1,0:T(8,128)(2,1)S(1)}, bf16[48,4096]{1,0:T(8,128)(2,1)S(1)}, u32[]{:S(2)}, u32[]{:S(2)}) collective-permute-start(bf16[48,4096]{1,0:T(8,128)(2,1)S(1)} %slice_add_fusion.24), channel_id=1, source_target_pairs={{0,2},{1,3},{6,4},{7,5},{8,10},{9,11},{14,12},{15,13},{16,18},{17,... | collective-permute-start | bytes 1179656 | tf_op jit(solution)/shard_map/ppermute | solution.py:154
  383.5 17.0 %copy-start.7 = (bf16[64,4096]{1,0:T(8,128)(2,1)S(1)}, bf16[64,4096]{1,0:T(8,128)(2,1)}, u32[]{:S(2)}) copy-start(bf16[64,4096]{1,0:T(8,128)(2,1)} %slice_add_fusion.18) | copy-start | bytes 1572868
  398.3 12.6 %collective-permute-start.48 = (bf16[48,4096]{1,0:T(8,128)(2,1)S(1)}, bf16[48,4096]{1,0:T(8,128)(2,1)S(1)}, u32[]{:S(2)}, u32[]{:S(2)}) collective-permute-start(bf16[48,4096]{1,0:T(8,128)(2,1)S(1)} %slice_add_fusion.28), channel_id=1, source_target_pairs={{2,0},{3,1},{4,6},{5,7},{10,8},{11,9},{12,14},{13,15},{18,16},{19,... | collective-permute-start | bytes 1179656 | tf_op jit(solution)/shard_map/ppermute | solution.py:174
  399.7 11.3 %collective-permute-start.49 = (bf16[64,4096]{1,0:T(8,128)(2,1)S(1)}, bf16[64,4096]{1,0:T(8,128)(2,1)S(1)}, u32[]{:S(2)}, u32[]{:S(2)}) collective-permute-start(bf16[64,4096]{1,0:T(8,128)(2,1)S(1)} %slice_add_fusion.17), channel_id=1, source_target_pairs={{2,4},{3,5},{4,2},{5,3},{10,12},{11,13},{12,10},{13,11},{18,20},{1... | collective-permute-start | bytes 1572872 | tf_op jit(solution)/shard_map/ppermute | solution.py:169
  402.2 10.8 %copy-start.11 = (bf16[48,4096]{1,0:T(8,128)(2,1)S(1)}, bf16[48,4096]{1,0:T(8,128)(2,1)}, u32[]{:S(2)}) copy-start(bf16[48,4096]{1,0:T(8,128)(2,1)} %slice_add_fusion.25) | copy-start | bytes 1179652
  411.0 13.0 %collective-permute-start.50 = (bf16[32,4096]{1,0:T(8,128)(2,1)S(1)}, bf16[32,4096]{1,0:T(8,128)(2,1)S(1)}, u32[]{:S(2)}, u32[]{:S(2)}) collective-permute-start(bf16[32,4096]{1,0:T(8,128)(2,1)S(1)} %slice_add_fusion.31), channel_id=1, source_target_pairs={{2,0},{3,1},{4,6},{5,7},{10,8},{11,9},{12,14},{13,15},{18,16},{19,... | collective-permute-start | bytes 786440 | tf_op jit(solution)/shard_map/ppermute | solution.py:174
  412.3 11.6 %collective-permute-start.52 = (bf16[32,4096]{1,0:T(8,128)(2,1)S(1)}, bf16[32,4096]{1,0:T(8,128)(2,1)S(1)}, u32[]{:S(2)}, u32[]{:S(2)}) collective-permute-start(bf16[32,4096]{1,0:T(8,128)(2,1)S(1)} %slice_add_fusion.29), channel_id=1, source_target_pairs={{2,4},{3,5},{4,2},{5,3},{10,12},{11,13},{12,10},{13,11},{18,20},{1... | collective-permute-start | bytes 786440 | tf_op jit(solution)/shard_map/ppermute | solution.py:169
  413.0 20.6 %copy-start.1 = (bf16[896,896]{1,0:T(8,128)(2,1)S(1)}, bf16[896,896]{1,0:T(8,128)(2,1)}, u32[]{:S(2)}) copy-start(bf16[896,896]{1,0:T(8,128)(2,1)} %param.15) | copy-start | bytes 4816900
  424.0 7.9 %collective-permute-start.53 = (bf16[16,4096]{1,0:T(8,128)(2,1)S(1)}, bf16[16,4096]{1,0:T(8,128)(2,1)S(1)}, u32[]{:S(2)}, u32[]{:S(2)}) collective-permute-start(bf16[16,4096]{1,0:T(8,128)(2,1)S(1)} %slice_add_fusion.33), channel_id=1, source_target_pairs={{2,0},{3,1},{4,6},{5,7},{10,8},{11,9},{12,14},{13,15},{18,16},{19,... | collective-permute-start | bytes 393224 | tf_op jit(solution)/shard_map/ppermute | solution.py:174
  (22 other events, 87.5 us)

commit v2 on v1

--- a/solution.py
+++ b/solution.py
@@ -31,11 +31,7 @@
 
 
 def add_throats(child_update, pivots, pores, values):
-    high = lax.reduce_precision(values, 8, 7)
-    low = values - high
-    values = jnp.concatenate([high, low]).astype(jnp.bfloat16)
-    pivots = jnp.concatenate([pivots, pivots])
-    pores = jnp.concatenate([pores, pores])
+    values = values.astype(jnp.bfloat16)
     rows = jnp.arange(child_update.shape[0], dtype=jnp.int32)
     columns = jnp.arange(child_update.shape[1], dtype=jnp.int32)
     left = jnp.where(rows[:, None] == pivots[None, :], values[None, :], jnp.bfloat16(0))

time: 442 us -> 441 us (level)
  starting transfers between devices: 101 us -> 95.8 us
    dot_general x1 -> x0, matrix products: 13.9 us -> none  [add_throats(): summed = jnp.dot(left, right, preferred_element_type=jnp.float32)]
    dot_general x1, matrix products: 9.14 us -> 17.4 us  [per_device(): jnp.dot(interior_inverse, coupling, preferred_element_type=jnp.float32)]
  transfers between devices with their start and end apart: 55 -> 55, of which waited for: 22 -> 25; matrix products, arithmetic and copies ran while one was open for 33% -> 33% of each run, Pallas kernels for 0% -> 0%
where the time goes in v2:
time: 441 us; the launch traced here: 433 us
  waiting for transfers between devices  153 us (35%)
  matrix products  122 us (28%)
  starting transfers between devices  95.8 us (22%)
  other arithmetic  56.3 us (13%)
  local copies, waits for them, and re-layouts  4.46 us (1%)
    dot_general x20, matrix products, multiply(): jnp.dot(picked, shared['solved'], preferred_element_type=jnp.float32)  61.6 us
    ppermute x10, waiting for transfers between devices, share_again(): s['rows_in'] = lax.ppermute(s['rows'], 'row', along_y)  57.3 us
    ppermute x10, starting transfers between devices, move_in(): come = lax.ppermute(sent, 'col', ends if k < count - ALONE else inward)  48.9 us
    dot_general x10, matrix products, pick(): lax.dot_general(onehot, shared['solved'], (((1,), (1,)), ((), ())), prefe...  42.5 us
    ppermute x4, waiting for transfers between devices, move_out(): s['from_inner'] = lax.ppermute(leaving(k), 'col', outward)  38.7 us
    ppermute x10, waiting for transfers between devices, move_in(): come = lax.ppermute(sent, 'col', ends if k < count - ALONE else inward)  32.9 us
    ppermute x10, waiting for transfers between devices, share(): s['rows_in'] = lax.ppermute(s['rows'], 'row', along_x)  22.7 us
    dot_general x1, matrix products, per_device(): jnp.dot(interior_inverse, coupling, preferred_element_type=jnp.float32)  17.4 us
  transfers between devices with their start and end apart: 55, of which 25 were waited for; matrix products, arithmetic and copies ran while one was open for 33% of the time, Pallas kernels for 0%

profile of v2, /device:TPU:0, one launch (start us, length us, event | category | flops | bytes accessed | tf_op | source)
XLA Modules:
  0.0 432.5 jit_solution(2915739548231446492)
XLA Ops:
  2.1 5.2 %all-to-all-start = ((f32[4,2,128]{2,1,0:T(2,128)}), f32[4,2,128]{2,1,0:T(2,128)S(1)}, u32[]{:S(2)}, u32[]{:S(2)}) async-start(f32[4,2,128]{2,1,0:T(2,128)} %pad_maximum_fusion.6), calls=%async_computation | async-start | bytes 8192 | tf_op jit(solution)/shard_map/all_to_all | solution.py:27
  12.0 17.4 %convert_bitcast_fusion = bf16[896,4096]{0,1:T(8,128)(2,1)} fusion(bf16[896,896]{1,0:T(8,128)(2,1)S(1)} %copy-done, bf16[896,4096]{1,0:T(8,128)(2,1)} %param.13, s32[512]{0:T(512)S(1)} %get-tuple-element.496, s32[512]{0:T(512)S(1)} %get-tuple-element.495, bf16[512]{0:T(512)(128)(2,1)S(1)} %bitcast.55), kind=kOutput, calls=%fused_computation.15 | convolution fusion | flops 10352459776 | bytes 16290816 | tf_op jit(solution)/shard_map/dot_general | solution.py:74
  29.3 6.7 %fusion.30 = bf16[384,896]{1,0:T(8,128)(2,1)S(1)} fusion(bf16[896,4096]{0,1:T(8,128)(2,1)} %convert_bitcast_fusion, s32[384]{0:T(512)S(1)} %pad_add_fusion), kind=kOutput, calls=%fused_computation.74 | convolution fusion | flops 2820489216 | bytes 8029696 | tf_op jit(solution)/shard_map/dot_general | solution.py:103
  36.7 3.5 fusion.29
  40.1 11.7 %collective-permute-done = bf16[384,896]{1,0:T(8,128)(2,1)S(1)} collective-permute-done((bf16[384,896]{1,0:T(8,128)(2,1)S(1)}, bf16[384,896]{1,0:T(8,128)(2,1)S(1)}, u32[]{:S(2)}, u32[]{:S(2)}) %collective-permute-start) | collective-permute-done | bytes 688160 | tf_op jit(solution)/shard_map/ppermute | solution.py:110
  54.9 4.5 %fusion.27 = bf16[512,896]{1,0:T(8,128)(2,1)S(1)} fusion(bf16[896,4096]{0,1:T(8,128)(2,1)S(1)} %copy-done.2, s32[512]{0:T(512)S(1)} %pad_add_fusion.2), kind=kOutput, calls=%fused_computation.71 | convolution fusion | flops 3760652288 | bytes 8259584 | tf_op jit(solution)/shard_map/dot_general | solution.py:103
  59.5 7.9 %collective-permute-done.1 = bf16[384,896]{1,0:T(8,128)(2,1)S(1)} collective-permute-done((bf16[384,896]{1,0:T(8,128)(2,1)S(1)}, bf16[384,896]{1,0:T(8,128)(2,1)S(1)}, u32[]{:S(2)}, u32[]{:S(2)}) %collective-permute-start.1) | collective-permute-done | bytes 688160 | tf_op jit(solution)/shard_map/ppermute | solution.py:118
  69.0 2.6 convolution_convert_fusion.14
  74.0 2.6 convolution_convert_fusion.15
  76.6 4.8 %fusion.26 = bf16[512,896]{1,0:T(8,128)(2,1)S(1)} fusion(bf16[896,4096]{0,1:T(8,128)(2,1)S(1)} %copy-done.2, s32[512]{0:T(512)S(1)} %pad_add_fusion.3), kind=kOutput, calls=%fused_computation.70 | convolution fusion | flops 3760652288 | bytes 8259584 | tf_op jit(solution)/shard_map/dot_general | solution.py:103
  81.6 8.3 %collective-permute-done.4 = bf16[384,896]{1,0:T(8,128)(2,1)S(1)} collective-permute-done((bf16[384,896]{1,0:T(8,128)(2,1)S(1)}, bf16[384,896]{1,0:T(8,128)(2,1)S(1)}, u32[]{:S(2)}, u32[]{:S(2)}) %collective-permute-start.4) | collective-permute-done | bytes 688160 | tf_op jit(solution)/shard_map/ppermute | solution.py:118
  89.8 5.0 %collective-permute-done.5 = bf16[512,896]{1,0:T(8,128)(2,1)S(1)} collective-permute-done((bf16[512,896]{1,0:T(8,128)(2,1)S(1)}, bf16[512,896]{1,0:T(8,128)(2,1)S(1)}, u32[]{:S(2)}, u32[]{:S(2)}) %collective-permute-start.5) | collective-permute-done | bytes 917536 | tf_op jit(solution)/shard_map/ppermute | solution.py:110
  95.0 2.6 convolution_convert_fusion.12
  102.7 2.6 convolution_convert_fusion.13
  105.3 4.5 %fusion.25 = bf16[512,896]{1,0:T(8,128)(2,1)S(1)} fusion(bf16[896,4096]{0,1:T(8,128)(2,1)S(1)} %copy-done.2, s32[512]{0:T(512)S(1)} %pad_add_fusion.4), kind=kOutput, calls=%fused_computation.69 | convolution fusion | flops 3760652288 | bytes 8259584 | tf_op jit(solution)/shard_map/dot_general | solution.py:103
  110.8 11.2 %collective-permute-done.8 = bf16[512,896]{1,0:T(8,128)(2,1)S(1)} collective-permute-done((bf16[512,896]{1,0:T(8,128)(2,1)S(1)}, bf16[512,896]{1,0:T(8,128)(2,1)S(1)}, u32[]{:S(2)}, u32[]{:S(2)}) %collective-permute-start.8) | collective-permute-done | bytes 917536 | tf_op jit(solution)/shard_map/ppermute | solution.py:118
  123.4 2.7 collective-permute-done.6
  126.3 4.1 convolution_convert_fusion.8
  130.8 1.7 collective-permute-start.11
  135.6 2.4 convolution_convert_fusion.9
  137.9 4.5 %fusion.24 = bf16[512,896]{1,0:T(8,128)(2,1)S(1)} fusion(bf16[896,4096]{0,1:T(8,128)(2,1)S(1)} %copy-done.2, s32[512]{0:T(512)S(1)} %pad_add_fusion.5), kind=kOutput, calls=%fused_computation.68 | convolution fusion | flops 3760652288 | bytes 8259584 | tf_op jit(solution)/shard_map/dot_general | solution.py:103
  143.5 10.1 %collective-permute-done.11 = bf16[512,896]{1,0:T(8,128)(2,1)S(1)} collective-permute-done((bf16[512,896]{1,0:T(8,128)(2,1)S(1)}, bf16[512,896]{1,0:T(8,128)(2,1)S(1)}, u32[]{:S(2)}, u32[]{:S(2)}) %collective-permute-start.11) | collective-permute-done | bytes 917536 | tf_op jit(solution)/shard_map/ppermute | solution.py:118
  155.2 3.7 convolution_convert_fusion.6
  163.9 2.4 convolution_convert_fusion.7
  166.3 4.5 %fusion.23 = bf16[512,896]{1,0:T(8,128)(2,1)S(1)} fusion(bf16[896,4096]{0,1:T(8,128)(2,1)S(1)} %copy-done.2, s32[512]{0:T(512)S(1)} %pad_add_fusion.6), kind=kOutput, calls=%fused_computation.67 | convolution fusion | flops 3760652288 | bytes 8259584 | tf_op jit(solution)/shard_map/dot_general | solution.py:103
  170.8 3.6 collective-permute-start.22
  174.7 10.0 %collective-permute-done.15 = bf16[512,896]{1,0:T(8,128)(2,1)S(1)} collective-permute-done((bf16[512,896]{1,0:T(8,128)(2,1)S(1)}, bf16[512,896]{1,0:T(8,128)(2,1)S(1)}, u32[]{:S(2)}, u32[]{:S(2)}) %collective-permute-start.15) | collective-permute-done | bytes 917536 | tf_op jit(solution)/shard_map/ppermute | solution.py:118
  187.9 3.7 convolution_convert_fusion.4
  197.5 2.4 convolution_convert_fusion.5
  199.9 4.3 %fusion.28 = bf16[384,896]{1,0:T(8,128)(2,1)} fusion(bf16[896,4096]{0,1:T(8,128)(2,1)S(1)} %copy-done.2, s32[384]{0:T(512)S(1)} %pad_add_fusion.7), kind=kOutput, calls=%fused_computation.72 | convolution fusion | flops 2820489216 | bytes 8029696 | tf_op jit(solution)/shard_map/dot_general | solution.py:103
  204.2 4.1 collective-permute-start.27
  209.3 5.3 %collective-permute-done.20 = bf16[512,896]{1,0:T(8,128)(2,1)S(1)} collective-permute-done((bf16[512,896]{1,0:T(8,128)(2,1)S(1)}, bf16[512,896]{1,0:T(8,128)(2,1)S(1)}, u32[]{:S(2)}, u32[]{:S(2)}) %collective-permute-start.20) | collective-permute-done | bytes 917536 | tf_op jit(solution)/shard_map/ppermute | solution.py:118
  217.3 3.7 convolution_convert_fusion.2
  225.9 2.4 convolution_convert_fusion.3
  228.3 3.2 fusion.31
  231.4 6.8 %collective-permute-start.32 = (bf16[192,4096]{1,0:T(8,128)(2,1)}, bf16[192,4096]{1,0:T(8,128)(2,1)S(1)}, u32[]{:S(2)}, u32[]{:S(2)}) collective-permute-start(bf16[192,4096]{1,0:T(8,128)(2,1)} %pad_maximum_fusion.1), channel_id=1, source_target_pairs={{0,2},{1,3},{2,0},{3,1},{4,6},{5,7},{6,4},{7,5},{8,10},{9,11},{10,... | collective-permute-start | bytes 4718600 | tf_op jit(solution)/shard_map/ppermute | solution.py:150
  239.6 4.5 %collective-permute-done.25 = bf16[512,896]{1,0:T(8,128)(2,1)S(1)} collective-permute-done((bf16[512,896]{1,0:T(8,128)(2,1)S(1)}, bf16[512,896]{1,0:T(8,128)(2,1)S(1)}, u32[]{:S(2)}, u32[]{:S(2)}) %collective-permute-start.25) | collective-permute-done | bytes 917536 | tf_op jit(solution)/shard_map/ppermute | solution.py:118
  245.3 2.1 collective-permute-start.28
  247.7 3.7 convolution_convert_fusion
  255.0 2.0 fusion.32
  258.5 5.1 %convolution_convert_fusion.1 = bf16[256,4096]{1,0:T(8,128)(2,1)} fusion(bf16[896,4096]{0,1:T(8,128)(2,1)S(1)} %copy-done.2, bf16[512,896]{1,0:T(8,128)(2,1)} %copy-done.19), kind=kOutput, calls=%fused_computation.23 | convolution fusion | flops 1880096768 | bytes 9895936 | tf_op jit(solution)/shard_map/dot_general | solution.py:127
  265.3 7.6 %collective-permute-start.37 = (bf16[192,4096]{1,0:T(8,128)(2,1)}, bf16[192,4096]{1,0:T(8,128)(2,1)S(1)}, u32[]{:S(2)}, u32[]{:S(2)}) collective-permute-start(bf16[192,4096]{1,0:T(8,128)(2,1)} %pad_maximum_fusion.2), channel_id=1, source_target_pairs={{0,2},{1,3},{2,0},{3,1},{4,6},{5,7},{6,4},{7,5},{8,10},{9,11},{10,... | collective-permute-start | bytes 4718600 | tf_op jit(solution)/shard_map/ppermute | solution.py:150
  274.5 1.9 slice_add_fusion.18
  278.9 1.8 collective-permute-start.33
  282.0 3.8 convolution_convert_fusion.10
  285.8 2.0 add.356
  291.4 2.6 convolution_convert_fusion.11
  295.7 3.8 collective-permute-start.41
  300.9 1.8 slice_add_fusion.25
  304.0 3.4 convolution_convert_fusion.16
  307.4 2.5 convolution_convert_fusion.17
  315.2 5.5 %collective-permute-start.44 = (bf16[144,4096]{1,0:T(8,128)(2,1)S(1)}, bf16[144,4096]{1,0:T(8,128)(2,1)S(1)}, u32[]{:S(2)}, u32[]{:S(2)}) collective-permute-start(bf16[144,4096]{1,0:T(8,128)(2,1)S(1)} %pad_maximum_fusion.4), channel_id=1, source_target_pairs={{0,2},{1,3},{2,0},{3,1},{4,6},{5,7},{6,4},{7,5},{8,10},{9,11},{10,... | collective-permute-start | bytes 3538952 | tf_op jit(solution)/shard_map/ppermute | solution.py:150
  322.5 22.3 %collective-permute-done.41 = bf16[192,4096]{1,0:T(8,128)(2,1)S(1)} collective-permute-done((bf16[192,4096]{1,0:T(8,128)(2,1)}, bf16[192,4096]{1,0:T(8,128)(2,1)S(1)}, u32[]{:S(2)}, u32[]{:S(2)}) %collective-permute-start.41) | collective-permute-done | bytes 1572896 | tf_op jit(solution)/shard_map/ppermute | solution.py:150
  345.9 1.8 collective-permute-start.42
  347.8 3.2 convolution_convert_fusion.18
  352.1 3.9 collective-permute-start.47
  357.7 2.4 convolution_convert_fusion.19
  364.5 5.7 %collective-permute-done.44 = bf16[144,4096]{1,0:T(8,128)(2,1)S(1)} collective-permute-done((bf16[144,4096]{1,0:T(8,128)(2,1)S(1)}, bf16[144,4096]{1,0:T(8,128)(2,1)S(1)}, u32[]{:S(2)}, u32[]{:S(2)}) %collective-permute-start.44) | collective-permute-done | bytes 1179680 | tf_op jit(solution)/shard_map/ppermute | solution.py:150
  370.9 10.3 %collective-permute-start.51 = (bf16[48,4096]{1,0:T(8,128)(2,1)S(1)}, bf16[48,4096]{1,0:T(8,128)(2,1)S(1)}, u32[]{:S(2)}, u32[]{:S(2)}) collective-permute-start(bf16[48,4096]{1,0:T(8,128)(2,1)S(1)} %slice_add_fusion.24), channel_id=1, source_target_pairs={{0,2},{1,3},{6,4},{7,5},{8,10},{9,11},{14,12},{15,13},{16,18},{17,... | collective-permute-start | bytes 1179656 | tf_op jit(solution)/shard_map/ppermute | solution.py:150
  381.3 1.8 subtract_dynamic-update-slice_fusion.1
  383.1 14.4 %collective-permute-done.45 = bf16[64,4096]{1,0:T(8,128)(2,1)S(1)} collective-permute-done((bf16[64,4096]{1,0:T(8,128)(2,1)S(1)}, bf16[64,4096]{1,0:T(8,128)(2,1)S(1)}, u32[]{:S(2)}, u32[]{:S(2)}) %collective-permute-start.45) | collective-permute-done | bytes 524320 | tf_op jit(solution)/shard_map/ppermute | solution.py:170
  402.0 7.8 %collective-permute-done.48 = bf16[48,4096]{1,0:T(8,128)(2,1)S(1)} collective-permute-done((bf16[48,4096]{1,0:T(8,128)(2,1)S(1)}, bf16[48,4096]{1,0:T(8,128)(2,1)S(1)}, u32[]{:S(2)}, u32[]{:S(2)}) %collective-permute-start.48) | collective-permute-done | bytes 393248 | tf_op jit(solution)/shard_map/ppermute | solution.py:170
  412.4 10.1 %collective-permute-done.50 = bf16[32,4096]{1,0:T(8,128)(2,1)S(1)} collective-permute-done((bf16[32,4096]{1,0:T(8,128)(2,1)S(1)}, bf16[32,4096]{1,0:T(8,128)(2,1)S(1)}, u32[]{:S(2)}, u32[]{:S(2)}) %collective-permute-start.50) | collective-permute-done | bytes 262176 | tf_op jit(solution)/shard_map/ppermute | solution.py:170
  424.2 6.3 %collective-permute-done.53 = bf16[16,4096]{1,0:T(8,128)(2,1)S(1)} collective-permute-done((bf16[16,4096]{1,0:T(8,128)(2,1)S(1)}, bf16[16,4096]{1,0:T(8,128)(2,1)S(1)}, u32[]{:S(2)}, u32[]{:S(2)}) %collective-permute-start.53) | collective-permute-done | bytes 131104 | tf_op jit(solution)/shard_map/ppermute | solution.py:170
  (270 shorter events, 100.5 us)
Async XLA Ops:
  0.0 12.0 %copy-start = (bf16[896,896]{1,0:T(8,128)(2,1)S(1)}, bf16[896,896]{1,0:T(8,128)(2,1)}, u32[]{:S(2)}) copy-start(bf16[896,896]{1,0:T(8,128)(2,1)} %param.15) | copy-start | bytes 4816900
  2.1 9.8 %all-to-all-start = ((f32[4,2,128]{2,1,0:T(2,128)}), f32[4,2,128]{2,1,0:T(2,128)S(1)}, u32[]{:S(2)}, u32[]{:S(2)}) async-start(f32[4,2,128]{2,1,0:T(2,128)} %pad_maximum_fusion.6), calls=%async_computation | async-start | bytes 8192 | tf_op jit(solution)/shard_map/all_to_all | solution.py:27
  36.0 15.8 %collective-permute-start = (bf16[384,896]{1,0:T(8,128)(2,1)S(1)}, bf16[384,896]{1,0:T(8,128)(2,1)S(1)}, u32[]{:S(2)}, u32[]{:S(2)}) collective-permute-start(bf16[384,896]{1,0:T(8,128)(2,1)S(1)} %fusion.30), channel_id=1, source_target_pairs={{0,8},{8,0},{16,24},{24,16},{1,9},{9,1},{17,25},{25,17},{2,10},{10... | collective-permute-start | bytes 2064392 | tf_op jit(solution)/shard_map/ppermute | solution.py:110
  52.0 15.4 %collective-permute-start.1 = (bf16[384,896]{1,0:T(8,128)(2,1)S(1)}, bf16[384,896]{1,0:T(8,128)(2,1)S(1)}, u32[]{:S(2)}, u32[]{:S(2)}) collective-permute-start(bf16[384,896]{1,0:T(8,128)(2,1)S(1)} %add.313), channel_id=1, source_target_pairs={{0,16},{8,24},{16,0},{24,8},{1,17},{9,25},{17,1},{25,9},{2,18},{10... | collective-permute-start | bytes 2064392 | tf_op jit(solution)/shard_map/ppermute | solution.py:118
  53.5 15.4 %collective-permute-start.2 = (bf16[384,896]{1,0:T(8,128)(2,1)S(1)}, bf16[384,896]{1,0:T(8,128)(2,1)S(1)}, u32[]{:S(2)}, u32[]{:S(2)}) collective-permute-start(bf16[384,896]{1,0:T(8,128)(2,1)S(1)} %fusion.29), channel_id=1, source_target_pairs={{0,8},{8,0},{16,24},{24,16},{1,9},{9,1},{17,25},{25,17},{2,10},{10... | collective-permute-start | bytes 2064392 | tf_op jit(solution)/shard_map/ppermute | solution.py:110
  71.6 9.7 %collective-permute-start.3 = (bf16[192,4096]{1,0:T(8,128)(2,1)S(1)}, bf16[192,4096]{1,0:T(8,128)(2,1)S(1)}, u32[]{:S(2)}, u32[]{:S(2)}) collective-permute-start(bf16[192,4096]{1,0:T(8,128)(2,1)S(1)} %convolution_convert_fusion.14), channel_id=1, source_target_pairs={{0,1},{1,0},{2,3},{3,2},{4,5},{5,4},{6,7},{7,6},{8,9},{9,8},{10,11... | collective-permute-start | bytes 4718600 | tf_op jit(solution)/shard_map/ppermute | solution.py:131
  71.9 17.9 %collective-permute-start.4 = (bf16[384,896]{1,0:T(8,128)(2,1)S(1)}, bf16[384,896]{1,0:T(8,128)(2,1)S(1)}, u32[]{:S(2)}, u32[]{:S(2)}) collective-permute-start(bf16[384,896]{1,0:T(8,128)(2,1)S(1)} %add.317), channel_id=1, source_target_pairs={{0,16},{8,24},{16,0},{24,8},{1,17},{9,25},{17,1},{25,9},{2,18},{10... | collective-permute-start | bytes 2064392 | tf_op jit(solution)/shard_map/ppermute | solution.py:118
  72.3 22.5 %collective-permute-start.5 = (bf16[512,896]{1,0:T(8,128)(2,1)S(1)}, bf16[512,896]{1,0:T(8,128)(2,1)S(1)}, u32[]{:S(2)}, u32[]{:S(2)}) collective-permute-start(bf16[512,896]{1,0:T(8,128)(2,1)S(1)} %fusion.27), channel_id=1, source_target_pairs={{0,8},{8,0},{16,24},{24,16},{1,9},{9,1},{17,25},{25,17},{2,10},{10... | collective-permute-start | bytes 2752520 | tf_op jit(solution)/shard_map/ppermute | solution.py:110
  97.6 12.3 %collective-permute-start.7 = (bf16[192,4096]{1,0:T(8,128)(2,1)S(1)}, bf16[192,4096]{1,0:T(8,128)(2,1)S(1)}, u32[]{:S(2)}, u32[]{:S(2)}) collective-permute-start(bf16[192,4096]{1,0:T(8,128)(2,1)S(1)} %convolution_convert_fusion.12), channel_id=1, source_target_pairs={{0,1},{1,0},{2,3},{3,2},{4,5},{5,4},{6,7},{7,6},{8,9},{9,8},{10,11... | collective-permute-start | bytes 4718600 | tf_op jit(solution)/shard_map/ppermute | solution.py:131
  97.7 28.4 %collective-permute-start.6 = (bf16[144,4096]{1,0:T(8,128)(2,1)S(1)}, bf16[144,4096]{1,0:T(8,128)(2,1)S(1)}, u32[]{:S(2)}, u32[]{:S(2)}) collective-permute-start(bf16[144,4096]{1,0:T(8,128)(2,1)S(1)} %slice_add_fusion.7), channel_id=1, source_target_pairs={{0,2},{1,3},{2,0},{3,1},{4,6},{5,7},{6,4},{7,5},{8,10},{9,11},{10,... | collective-permute-start | bytes 3538952 | tf_op jit(solution)/shard_map/ppermute | solution.py:150
  99.5 22.5 %collective-permute-start.8 = (bf16[512,896]{1,0:T(8,128)(2,1)S(1)}, bf16[512,896]{1,0:T(8,128)(2,1)S(1)}, u32[]{:S(2)}, u32[]{:S(2)}) collective-permute-start(bf16[512,896]{1,0:T(8,128)(2,1)S(1)} %add.321), channel_id=1, source_target_pairs={{0,16},{8,24},{16,0},{24,8},{1,17},{9,25},{17,1},{25,9},{2,18},{10... | collective-permute-start | bytes 2752520 | tf_op jit(solution)/shard_map/ppermute | solution.py:118
  101.2 22.1 %collective-permute-start.9 = (bf16[512,896]{1,0:T(8,128)(2,1)S(1)}, bf16[512,896]{1,0:T(8,128)(2,1)S(1)}, u32[]{:S(2)}, u32[]{:S(2)}) collective-permute-start(bf16[512,896]{1,0:T(8,128)(2,1)S(1)} %fusion.26), channel_id=1, source_target_pairs={{0,8},{8,0},{16,24},{24,16},{1,9},{9,1},{17,25},{25,17},{2,10},{10... | collective-permute-start | bytes 2752520 | tf_op jit(solution)/shard_map/ppermute | solution.py:110
  126.0 32.9 %copy-start.13 = (bf16[144,4096]{1,0:T(8,128)(2,1)}, bf16[144,4096]{1,0:T(8,128)(2,1)S(1)}, u32[]{:S(2)}) copy-start(bf16[144,4096]{1,0:T(8,128)(2,1)S(1)} %collective-permute-done.6) | copy-start | bytes 3538948
  130.4 12.1 %collective-permute-start.10 = (bf16[256,4096]{1,0:T(8,128)(2,1)}, bf16[256,4096]{1,0:T(8,128)(2,1)S(1)}, u32[]{:S(2)}, u32[]{:S(2)}) collective-permute-start(bf16[256,4096]{1,0:T(8,128)(2,1)} %convolution_convert_fusion.8), channel_id=1, source_target_pairs={{0,1},{1,0},{2,3},{3,2},{4,5},{5,4},{6,7},{7,6},{8,9},{9,8},{10,11... | collective-permute-start | bytes 6291464 | tf_op jit(solution)/shard_map/ppermute | solution.py:131
  130.8 22.8 %collective-permute-start.11 = (bf16[512,896]{1,0:T(8,128)(2,1)S(1)}, bf16[512,896]{1,0:T(8,128)(2,1)S(1)}, u32[]{:S(2)}, u32[]{:S(2)}) collective-permute-start(bf16[512,896]{1,0:T(8,128)(2,1)S(1)} %add.325), channel_id=1, source_target_pairs={{0,16},{8,24},{16,0},{24,8},{1,17},{9,25},{17,1},{25,9},{2,18},{10... | collective-permute-start | bytes 2752520 | tf_op jit(solution)/shard_map/ppermute | solution.py:118
  132.5 22.5 %collective-permute-start.12 = (bf16[512,896]{1,0:T(8,128)(2,1)S(1)}, bf16[512,896]{1,0:T(8,128)(2,1)S(1)}, u32[]{:S(2)}, u32[]{:S(2)}) collective-permute-start(bf16[512,896]{1,0:T(8,128)(2,1)S(1)} %fusion.25), channel_id=1, source_target_pairs={{0,8},{8,0},{16,24},{24,16},{1,9},{9,1},{17,25},{25,17},{2,10},{10... | collective-permute-start | bytes 2752520 | tf_op jit(solution)/shard_map/ppermute | solution.py:110
  134.0 50.8 %collective-permute-start.17 = (bf16[144,4096]{1,0:T(8,128)(2,1)S(1)}, bf16[144,4096]{1,0:T(8,128)(2,1)S(1)}, u32[]{:S(2)}, u32[]{:S(2)}) collective-permute-start(bf16[144,4096]{1,0:T(8,128)(2,1)S(1)} %slice_add_fusion.6), channel_id=1, source_target_pairs={{0,2},{1,3},{2,0},{3,1},{4,6},{5,7},{6,4},{7,5},{8,10},{9,11},{10,... | collective-permute-start | bytes 3538952 | tf_op jit(solution)/shard_map/ppermute | solution.py:150
  158.9 11.9 %collective-permute-start.14 = (bf16[256,4096]{1,0:T(8,128)(2,1)}, bf16[256,4096]{1,0:T(8,128)(2,1)S(1)}, u32[]{:S(2)}, u32[]{:S(2)}) collective-permute-start(bf16[256,4096]{1,0:T(8,128)(2,1)} %convolution_convert_fusion.6), channel_id=1, source_target_pairs={{0,1},{1,0},{2,3},{3,2},{4,5},{5,4},{6,7},{7,6},{8,9},{9,8},{10,11... | collective-permute-start | bytes 6291464 | tf_op jit(solution)/shard_map/ppermute | solution.py:131
  159.9 14.8 %collective-permute-start.13 = (bf16[96,4096]{1,0:T(8,128)(2,1)}, bf16[96,4096]{1,0:T(8,128)(2,1)}, u32[]{:S(2)}, u32[]{:S(2)}) collective-permute-start(bf16[96,4096]{1,0:T(8,128)(2,1)} %slice_add_fusion.16), channel_id=1, source_target_pairs={{2,4},{3,5},{4,2},{5,3},{10,12},{11,13},{12,10},{13,11},{18,20},{1... | collective-permute-start | bytes 2359304 | tf_op jit(solution)/shard_map/ppermute | solution.py:165
  161.8 22.8 %collective-permute-start.15 = (bf16[512,896]{1,0:T(8,128)(2,1)S(1)}, bf16[512,896]{1,0:T(8,128)(2,1)S(1)}, u32[]{:S(2)}, u32[]{:S(2)}) collective-permute-start(bf16[512,896]{1,0:T(8,128)(2,1)S(1)} %add.330), channel_id=1, source_target_pairs={{0,16},{8,24},{16,0},{24,8},{1,17},{9,25},{17,1},{25,9},{2,18},{10... | collective-permute-start | bytes 2752520 | tf_op jit(solution)/shard_map/ppermute | solution.py:118
  162.3 22.5 %collective-permute-start.16 = (bf16[512,896]{1,0:T(8,128)(2,1)S(1)}, bf16[512,896]{1,0:T(8,128)(2,1)S(1)}, u32[]{:S(2)}, u32[]{:S(2)}) collective-permute-start(bf16[512,896]{1,0:T(8,128)(2,1)S(1)} %fusion.24), channel_id=1, source_target_pairs={{0,8},{8,0},{16,24},{24,16},{1,9},{9,1},{17,25},{25,17},{2,10},{10... | collective-permute-start | bytes 2752520 | tf_op jit(solution)/shard_map/ppermute | solution.py:110
  170.8 45.2 %collective-permute-start.22 = (bf16[192,4096]{1,0:T(8,128)(2,1)S(1)}, bf16[192,4096]{1,0:T(8,128)(2,1)S(1)}, u32[]{:S(2)}, u32[]{:S(2)}) collective-permute-start(bf16[192,4096]{1,0:T(8,128)(2,1)S(1)} %slice_add_fusion.4), channel_id=1, source_target_pairs={{0,2},{1,3},{2,0},{3,1},{4,6},{5,7},{6,4},{7,5},{8,10},{9,11},{10,... | collective-permute-start | bytes 4718600 | tf_op jit(solution)/shard_map/ppermute | solution.py:150
  185.9 23.4 %collective-permute-start.18 = (bf16[96,4096]{1,0:T(8,128)(2,1)}, bf16[96,4096]{1,0:T(8,128)(2,1)}, u32[]{:S(2)}, u32[]{:S(2)}) collective-permute-start(bf16[96,4096]{1,0:T(8,128)(2,1)} %slice_add_fusion.15), channel_id=1, source_target_pairs={{2,4},{3,5},{4,2},{5,3},{10,12},{11,13},{12,10},{13,11},{18,20},{1... | collective-permute-start | bytes 2359304 | tf_op jit(solution)/shard_map/ppermute | solution.py:165
  191.6 12.7 %collective-permute-start.19 = (bf16[256,4096]{1,0:T(8,128)(2,1)}, bf16[256,4096]{1,0:T(8,128)(2,1)S(1)}, u32[]{:S(2)}, u32[]{:S(2)}) collective-permute-start(bf16[256,4096]{1,0:T(8,128)(2,1)} %convolution_convert_fusion.4), channel_id=1, source_target_pairs={{0,1},{1,0},{2,3},{3,2},{4,5},{5,4},{6,7},{7,6},{8,9},{9,8},{10,11... | collective-permute-start | bytes 6291464 | tf_op jit(solution)/shard_map/ppermute | solution.py:131
  191.8 22.8 %collective-permute-start.20 = (bf16[512,896]{1,0:T(8,128)(2,1)S(1)}, bf16[512,896]{1,0:T(8,128)(2,1)S(1)}, u32[]{:S(2)}, u32[]{:S(2)}) collective-permute-start(bf16[512,896]{1,0:T(8,128)(2,1)S(1)} %add.335), channel_id=1, source_target_pairs={{0,16},{8,24},{16,0},{24,8},{1,17},{9,25},{17,1},{25,9},{2,18},{10... | collective-permute-start | bytes 2752520 | tf_op jit(solution)/shard_map/ppermute | solution.py:118
  193.5 22.5 %collective-permute-start.21 = (bf16[512,896]{1,0:T(8,128)(2,1)S(1)}, bf16[512,896]{1,0:T(8,128)(2,1)S(1)}, u32[]{:S(2)}, u32[]{:S(2)}) collective-permute-start(bf16[512,896]{1,0:T(8,128)(2,1)S(1)} %fusion.23), channel_id=1, source_target_pairs={{0,8},{8,0},{16,24},{24,16},{1,9},{9,1},{17,25},{25,17},{2,10},{10... | collective-permute-start | bytes 2752520 | tf_op jit(solution)/shard_map/ppermute | solution.py:110
  204.2 39.8 %collective-permute-start.27 = (bf16[192,4096]{1,0:T(8,128)(2,1)}, bf16[192,4096]{1,0:T(8,128)(2,1)S(1)}, u32[]{:S(2)}, u32[]{:S(2)}) collective-permute-start(bf16[192,4096]{1,0:T(8,128)(2,1)} %pad_maximum_fusion), channel_id=1, source_target_pairs={{0,2},{1,3},{2,0},{3,1},{4,6},{5,7},{6,4},{7,5},{8,10},{9,11},{10,... | collective-permute-start | bytes 4718600 | tf_op jit(solution)/shard_map/ppermute | solution.py:150
  216.1 28.0 %collective-permute-start.23 = (bf16[128,4096]{1,0:T(8,128)(2,1)S(1)}, bf16[128,4096]{1,0:T(8,128)(2,1)S(1)}, u32[]{:S(2)}, u32[]{:S(2)}) collective-permute-start(bf16[128,4096]{1,0:T(8,128)(2,1)S(1)} %slice_add_fusion.12), channel_id=1, source_target_pairs={{2,4},{3,5},{4,2},{5,3},{10,12},{11,13},{12,10},{13,11},{18,20},{1... | collective-permute-start | bytes 3145736 | tf_op jit(solution)/shard_map/ppermute | solution.py:165
  221.0 10.4 %collective-permute-start.24 = (bf16[256,4096]{1,0:T(8,128)(2,1)}, bf16[256,4096]{1,0:T(8,128)(2,1)S(1)}, u32[]{:S(2)}, u32[]{:S(2)}) collective-permute-start(bf16[256,4096]{1,0:T(8,128)(2,1)} %convolution_convert_fusion.2), channel_id=1, source_target_pairs={{0,1},{1,0},{2,3},{3,2},{4,5},{5,4},{6,7},{7,6},{8,9},{9,8},{10,11... | collective-permute-start | bytes 6291464 | tf_op jit(solution)/shard_map/ppermute | solution.py:131
  221.2 22.8 %collective-permute-start.25 = (bf16[512,896]{1,0:T(8,128)(2,1)S(1)}, bf16[512,896]{1,0:T(8,128)(2,1)S(1)}, u32[]{:S(2)}, u32[]{:S(2)}) collective-permute-start(bf16[512,896]{1,0:T(8,128)(2,1)S(1)} %add.340), channel_id=1, source_target_pairs={{0,16},{8,24},{16,0},{24,8},{1,17},{9,25},{17,1},{25,9},{2,18},{10... | collective-permute-start | bytes 2752520 | tf_op jit(solution)/shard_map/ppermute | solution.py:118
  221.7 17.9 %collective-permute-start.26 = (bf16[384,896]{1,0:T(8,128)(2,1)}, bf16[384,896]{1,0:T(8,128)(2,1)}, u32[]{:S(2)}, u32[]{:S(2)}) collective-permute-start(bf16[384,896]{1,0:T(8,128)(2,1)} %fusion.28), channel_id=1, source_target_pairs={{0,8},{8,0},{16,24},{24,16},{1,9},{9,1},{17,25},{25,17},{2,10},{10... | collective-permute-start | bytes 2064392 | tf_op jit(solution)/shard_map/ppermute | solution.py:110
  231.4 46.0 %collective-permute-start.32 = (bf16[192,4096]{1,0:T(8,128)(2,1)}, bf16[192,4096]{1,0:T(8,128)(2,1)S(1)}, u32[]{:S(2)}, u32[]{:S(2)}) collective-permute-start(bf16[192,4096]{1,0:T(8,128)(2,1)} %pad_maximum_fusion.1), channel_id=1, source_target_pairs={{0,2},{1,3},{2,0},{3,1},{4,6},{5,7},{6,4},{7,5},{8,10},{9,11},{10,... | collective-permute-start | bytes 4718600 | tf_op jit(solution)/shard_map/ppermute | solution.py:150
  244.1 10.8 %copy-start.15 = (bf16[128,4096]{1,0:T(8,128)(2,1)}, bf16[128,4096]{1,0:T(8,128)(2,1)S(1)}, u32[]{:S(2)}) copy-start(bf16[128,4096]{1,0:T(8,128)(2,1)S(1)} %collective-permute-done.23) | copy-start | bytes 3145732
  245.3 31.1 %collective-permute-start.28 = (bf16[128,4096]{1,0:T(8,128)(2,1)}, bf16[128,4096]{1,0:T(8,128)(2,1)}, u32[]{:S(2)}, u32[]{:S(2)}) collective-permute-start(bf16[128,4096]{1,0:T(8,128)(2,1)} %slice_add_fusion.11), channel_id=1, source_target_pairs={{2,4},{3,5},{4,2},{5,3},{10,12},{11,13},{12,10},{13,11},{18,20},{1... | collective-permute-start | bytes 3145736 | tf_op jit(solution)/shard_map/ppermute | solution.py:165
  251.3 14.0 %collective-permute-start.29 = (bf16[256,4096]{1,0:T(8,128)(2,1)}, bf16[256,4096]{1,0:T(8,128)(2,1)}, u32[]{:S(2)}, u32[]{:S(2)}) collective-permute-start(bf16[256,4096]{1,0:T(8,128)(2,1)} %convolution_convert_fusion), channel_id=1, source_target_pairs={{0,1},{1,0},{2,3},{3,2},{4,5},{5,4},{6,7},{7,6},{8,9},{9,8},{10,11... | collective-permute-start | bytes 6291464 | tf_op jit(solution)/shard_map/ppermute | solution.py:131
  252.8 23.6 %collective-permute-start.30 = (bf16[384,896]{1,0:T(8,128)(2,1)S(1)}, bf16[384,896]{1,0:T(8,128)(2,1)}, u32[]{:S(2)}, u32[]{:S(2)}) collective-permute-start(bf16[384,896]{1,0:T(8,128)(2,1)S(1)} %add.348), channel_id=1, source_target_pairs={{0,16},{8,24},{16,0},{24,8},{1,17},{9,25},{17,1},{25,9},{2,18},{10... | collective-permute-start | bytes 2064392 | tf_op jit(solution)/shard_map/ppermute | solution.py:118
  253.2 23.2 %collective-permute-start.31 = (bf16[256,896]{1,0:T(8,128)(2,1)}, bf16[256,896]{1,0:T(8,128)(2,1)}, u32[]{:S(2)}, u32[]{:S(2)}) collective-permute-start(bf16[256,896]{1,0:T(8,128)(2,1)} %fusion.31), channel_id=1, source_target_pairs={{0,8},{8,0},{16,24},{24,16},{1,9},{9,1},{17,25},{25,17},{2,10},{10... | collective-permute-start | bytes 1376264 | tf_op jit(solution)/shard_map/ppermute | solution.py:110
  263.6 9.3 %copy-start.9 = (bf16[256,4096]{1,0:T(8,128)(2,1)S(1)}, bf16[256,4096]{1,0:T(8,128)(2,1)}, u32[]{:S(2)}) copy-start(bf16[256,4096]{1,0:T(8,128)(2,1)} %convolution_convert_fusion.1) | copy-start | bytes 6291460
  265.3 45.8 %collective-permute-start.37 = (bf16[192,4096]{1,0:T(8,128)(2,1)}, bf16[192,4096]{1,0:T(8,128)(2,1)S(1)}, u32[]{:S(2)}, u32[]{:S(2)}) collective-permute-start(bf16[192,4096]{1,0:T(8,128)(2,1)} %pad_maximum_fusion.2), channel_id=1, source_target_pairs={{0,2},{1,3},{2,0},{3,1},{4,6},{5,7},{6,4},{7,5},{8,10},{9,11},{10,... | collective-permute-start | bytes 4718600 | tf_op jit(solution)/shard_map/ppermute | solution.py:150
  278.9 23.8 %collective-permute-start.33 = (bf16[128,4096]{1,0:T(8,128)(2,1)}, bf16[128,4096]{1,0:T(8,128)(2,1)}, u32[]{:S(2)}, u32[]{:S(2)}) collective-permute-start(bf16[128,4096]{1,0:T(8,128)(2,1)} %slice_add_fusion.10), channel_id=1, source_target_pairs={{2,4},{3,5},{4,2},{5,3},{10,12},{11,13},{12,10},{13,11},{18,20},{1... | collective-permute-start | bytes 3145736 | tf_op jit(solution)/shard_map/ppermute | solution.py:165
  285.8 9.9 %collective-permute-start.34 = (bf16[192,4096]{1,0:T(8,128)(2,1)}, bf16[192,4096]{1,0:T(8,128)(2,1)}, u32[]{:S(2)}, u32[]{:S(2)}) collective-permute-start(bf16[192,4096]{1,0:T(8,128)(2,1)} %convolution_convert_fusion.10), channel_id=1, source_target_pairs={{0,1},{1,0},{2,3},{3,2},{4,5},{5,4},{6,7},{7,6},{8,9},{9,8},{10,11... | collective-permute-start | bytes 4718600 | tf_op jit(solution)/shard_map/ppermute | solution.py:131
  287.8 14.9 %collective-permute-start.35 = (bf16[256,896]{1,0:T(8,128)(2,1)}, bf16[256,896]{1,0:T(8,128)(2,1)}, u32[]{:S(2)}, u32[]{:S(2)}) collective-permute-start(bf16[256,896]{1,0:T(8,128)(2,1)} %add.356), channel_id=1, source_target_pairs={{0,16},{8,24},{16,0},{24,8},{1,17},{9,25},{17,1},{25,9},{2,18},{10... | collective-permute-start | bytes 1376264 | tf_op jit(solution)/shard_map/ppermute | solution.py:118
  288.4 14.3 %collective-permute-start.36 = (bf16[128,896]{1,0:T(8,128)(2,1)}, bf16[128,896]{1,0:T(8,128)(2,1)}, u32[]{:S(2)}, u32[]{:S(2)}) collective-permute-start(bf16[128,896]{1,0:T(8,128)(2,1)} %fusion.32), channel_id=1, source_target_pairs={{0,8},{8,0},{16,24},{24,16},{1,9},{9,1},{17,25},{25,17},{2,10},{10... | collective-permute-start | bytes 688136 | tf_op jit(solution)/shard_map/ppermute | solution.py:110
  295.7 49.2 %collective-permute-start.41 = (bf16[192,4096]{1,0:T(8,128)(2,1)}, bf16[192,4096]{1,0:T(8,128)(2,1)S(1)}, u32[]{:S(2)}, u32[]{:S(2)}) collective-permute-start(bf16[192,4096]{1,0:T(8,128)(2,1)} %pad_maximum_fusion.3), channel_id=1, source_target_pairs={{0,2},{1,3},{2,0},{3,1},{4,6},{5,7},{6,4},{7,5},{8,10},{9,11},{10,... | collective-permute-start | bytes 4718600 | tf_op jit(solution)/shard_map/ppermute | solution.py:150
  311.2 11.3 %collective-permute-start.38 = (bf16[128,4096]{1,0:T(8,128)(2,1)S(1)}, bf16[128,4096]{1,0:T(8,128)(2,1)S(1)}, u32[]{:S(2)}, u32[]{:S(2)}) collective-permute-start(bf16[128,4096]{1,0:T(8,128)(2,1)S(1)} %slice_add_fusion.9), channel_id=1, source_target_pairs={{2,4},{3,5},{4,2},{5,3},{10,12},{11,13},{12,10},{13,11},{18,20},{1... | collective-permute-start | bytes 3145736 | tf_op jit(solution)/shard_map/ppermute | solution.py:165
  312.0 10.4 %collective-permute-start.39 = (bf16[128,4096]{1,0:T(8,128)(2,1)}, bf16[128,4096]{1,0:T(8,128)(2,1)S(1)}, u32[]{:S(2)}, u32[]{:S(2)}) collective-permute-start(bf16[128,4096]{1,0:T(8,128)(2,1)} %convolution_convert_fusion.16), channel_id=1, source_target_pairs={{0,1},{1,0},{2,3},{3,2},{4,5},{5,4},{6,7},{7,6},{8,9},{9,8},{10,11... | collective-permute-start | bytes 3145736 | tf_op jit(solution)/shard_map/ppermute | solution.py:131
  313.2 9.3 %collective-permute-start.40 = (bf16[128,896]{1,0:T(8,128)(2,1)S(1)}, bf16[128,896]{1,0:T(8,128)(2,1)S(1)}, u32[]{:S(2)}, u32[]{:S(2)}) collective-permute-start(bf16[128,896]{1,0:T(8,128)(2,1)S(1)} %add.364), channel_id=1, source_target_pairs={{0,16},{8,24},{16,0},{24,8},{1,17},{9,25},{17,1},{25,9},{2,18},{10... | collective-permute-start | bytes 688136 | tf_op jit(solution)/shard_map/ppermute | solution.py:118
  315.2 54.9 %collective-permute-start.44 = (bf16[144,4096]{1,0:T(8,128)(2,1)S(1)}, bf16[144,4096]{1,0:T(8,128)(2,1)S(1)}, u32[]{:S(2)}, u32[]{:S(2)}) collective-permute-start(bf16[144,4096]{1,0:T(8,128)(2,1)S(1)} %pad_maximum_fusion.4), channel_id=1, source_target_pairs={{0,2},{1,3},{2,0},{3,1},{4,6},{5,7},{6,4},{7,5},{8,10},{9,11},{10,... | collective-permute-start | bytes 3538952 | tf_op jit(solution)/shard_map/ppermute | solution.py:150
  322.5 22.3 %copy-start.17 = (bf16[128,4096]{1,0:T(8,128)(2,1)}, bf16[128,4096]{1,0:T(8,128)(2,1)S(1)}, u32[]{:S(2)}) copy-start(bf16[128,4096]{1,0:T(8,128)(2,1)S(1)} %collective-permute-done.38) | copy-start | bytes 3145732
  345.9 16.1 %collective-permute-start.42 = (bf16[128,4096]{1,0:T(8,128)(2,1)}, bf16[128,4096]{1,0:T(8,128)(2,1)}, u32[]{:S(2)}, u32[]{:S(2)}) collective-permute-start(bf16[128,4096]{1,0:T(8,128)(2,1)} %slice_add_fusion.8), channel_id=1, source_target_pairs={{2,4},{3,5},{4,2},{5,3},{10,12},{11,13},{12,10},{13,11},{18,20},{1... | collective-permute-start | bytes 3145736 | tf_op jit(solution)/shard_map/ppermute | solution.py:165
  351.0 9.0 %collective-permute-start.43 = (bf16[64,4096]{1,0:T(8,128)(2,1)}, bf16[64,4096]{1,0:T(8,128)(2,1)}, u32[]{:S(2)}, u32[]{:S(2)}) collective-permute-start(bf16[64,4096]{1,0:T(8,128)(2,1)} %convolution_convert_fusion.18), channel_id=1, source_target_pairs={{0,1},{1,0},{2,3},{3,2},{4,5},{5,4},{6,7},{7,6},{8,9},{9,8},{10,11... | collective-permute-start | bytes 1572872 | tf_op jit(solution)/shard_map/ppermute | solution.py:131
  352.1 46.8 %collective-permute-start.47 = (bf16[96,4096]{1,0:T(8,128)(2,1)}, bf16[96,4096]{1,0:T(8,128)(2,1)S(1)}, u32[]{:S(2)}, u32[]{:S(2)}) collective-permute-start(bf16[96,4096]{1,0:T(8,128)(2,1)} %pad_maximum_fusion.5), channel_id=1, source_target_pairs={{0,2},{1,3},{2,0},{3,1},{4,6},{5,7},{6,4},{7,5},{8,10},{9,11},{10,... | collective-permute-start | bytes 2359304 | tf_op jit(solution)/shard_map/ppermute | solution.py:150
  361.1 20.2 %copy-start.6 = (bf16[64,4096]{1,0:T(8,128)(2,1)S(1)}, bf16[64,4096]{1,0:T(8,128)(2,1)}, u32[]{:S(2)}) copy-start(bf16[64,4096]{1,0:T(8,128)(2,1)} %slice_add_fusion.20) | copy-start | bytes 1572868
  363.2 34.3 %collective-permute-start.45 = (bf16[64,4096]{1,0:T(8,128)(2,1)S(1)}, bf16[64,4096]{1,0:T(8,128)(2,1)S(1)}, u32[]{:S(2)}, u32[]{:S(2)}) collective-permute-start(bf16[64,4096]{1,0:T(8,128)(2,1)S(1)} %slice_add_fusion.23), channel_id=1, source_target_pairs={{2,0},{3,1},{4,6},{5,7},{10,8},{11,9},{12,14},{13,15},{18,16},{19,... | collective-permute-start | bytes 1572872 | tf_op jit(solution)/shard_map/ppermute | solution.py:170
  370.2 27.3 %collective-permute-start.46 = (bf16[96,4096]{1,0:T(8,128)(2,1)S(1)}, bf16[96,4096]{1,0:T(8,128)(2,1)S(1)}, u32[]{:S(2)}, u32[]{:S(2)}) collective-permute-start(bf16[96,4096]{1,0:T(8,128)(2,1)S(1)} %slice_add_fusion.13), channel_id=1, source_target_pairs={{2,4},{3,5},{4,2},{5,3},{10,12},{11,13},{12,10},{13,11},{18,20},{1... | collective-permute-start | bytes 2359304 | tf_op jit(solution)/shard_map/ppermute | solution.py:165
  370.9 40.3 %collective-permute-start.51 = (bf16[48,4096]{1,0:T(8,128)(2,1)S(1)}, bf16[48,4096]{1,0:T(8,128)(2,1)S(1)}, u32[]{:S(2)}, u32[]{:S(2)}) collective-permute-start(bf16[48,4096]{1,0:T(8,128)(2,1)S(1)} %slice_add_fusion.24), channel_id=1, source_target_pairs={{0,2},{1,3},{6,4},{7,5},{8,10},{9,11},{14,12},{15,13},{16,18},{17,... | collective-permute-start | bytes 1179656 | tf_op jit(solution)/shard_map/ppermute | solution.py:150
  383.1 16.7 %copy-start.8 = (bf16[64,4096]{1,0:T(8,128)(2,1)S(1)}, bf16[64,4096]{1,0:T(8,128)(2,1)}, u32[]{:S(2)}) copy-start(bf16[64,4096]{1,0:T(8,128)(2,1)} %slice_add_fusion.18) | copy-start | bytes 1572868
  397.6 12.3 %collective-permute-start.48 = (bf16[48,4096]{1,0:T(8,128)(2,1)S(1)}, bf16[48,4096]{1,0:T(8,128)(2,1)S(1)}, u32[]{:S(2)}, u32[]{:S(2)}) collective-permute-start(bf16[48,4096]{1,0:T(8,128)(2,1)S(1)} %slice_add_fusion.28), channel_id=1, source_target_pairs={{2,0},{3,1},{4,6},{5,7},{10,8},{11,9},{12,14},{13,15},{18,16},{19,... | collective-permute-start | bytes 1179656 | tf_op jit(solution)/shard_map/ppermute | solution.py:170
  398.9 10.9 %collective-permute-start.49 = (bf16[64,4096]{1,0:T(8,128)(2,1)S(1)}, bf16[64,4096]{1,0:T(8,128)(2,1)S(1)}, u32[]{:S(2)}, u32[]{:S(2)}) collective-permute-start(bf16[64,4096]{1,0:T(8,128)(2,1)S(1)} %slice_add_fusion.17), channel_id=1, source_target_pairs={{2,4},{3,5},{4,2},{5,3},{10,12},{11,13},{12,10},{13,11},{18,20},{1... | collective-permute-start | bytes 1572872 | tf_op jit(solution)/shard_map/ppermute | solution.py:165
  401.4 10.5 %copy-start.12 = (bf16[48,4096]{1,0:T(8,128)(2,1)S(1)}, bf16[48,4096]{1,0:T(8,128)(2,1)}, u32[]{:S(2)}) copy-start(bf16[48,4096]{1,0:T(8,128)(2,1)} %slice_add_fusion.25) | copy-start | bytes 1179652
  409.9 12.7 %collective-permute-start.50 = (bf16[32,4096]{1,0:T(8,128)(2,1)S(1)}, bf16[32,4096]{1,0:T(8,128)(2,1)S(1)}, u32[]{:S(2)}, u32[]{:S(2)}) collective-permute-start(bf16[32,4096]{1,0:T(8,128)(2,1)S(1)} %slice_add_fusion.31), channel_id=1, source_target_pairs={{2,0},{3,1},{4,6},{5,7},{10,8},{11,9},{12,14},{13,15},{18,16},{19,... | collective-permute-start | bytes 786440 | tf_op jit(solution)/shard_map/ppermute | solution.py:170
  411.3 11.3 %collective-permute-start.52 = (bf16[32,4096]{1,0:T(8,128)(2,1)S(1)}, bf16[32,4096]{1,0:T(8,128)(2,1)S(1)}, u32[]{:S(2)}, u32[]{:S(2)}) collective-permute-start(bf16[32,4096]{1,0:T(8,128)(2,1)S(1)} %slice_add_fusion.29), channel_id=1, source_target_pairs={{2,4},{3,5},{4,2},{5,3},{10,12},{11,13},{12,10},{13,11},{18,20},{1... | collective-permute-start | bytes 786440 | tf_op jit(solution)/shard_map/ppermute | solution.py:165
  412.0 20.3 %copy-start.1 = (bf16[896,896]{1,0:T(8,128)(2,1)S(1)}, bf16[896,896]{1,0:T(8,128)(2,1)}, u32[]{:S(2)}) copy-start(bf16[896,896]{1,0:T(8,128)(2,1)} %param.15) | copy-start | bytes 4816900
  422.6 7.9 %collective-permute-start.53 = (bf16[16,4096]{1,0:T(8,128)(2,1)S(1)}, bf16[16,4096]{1,0:T(8,128)(2,1)S(1)}, u32[]{:S(2)}, u32[]{:S(2)}) collective-permute-start(bf16[16,4096]{1,0:T(8,128)(2,1)S(1)} %slice_add_fusion.33), channel_id=1, source_target_pairs={{2,0},{3,1},{4,6},{5,7},{10,8},{11,9},{12,14},{13,15},{18,16},{19,... | collective-permute-start | bytes 393224 | tf_op jit(solution)/shard_map/ppermute | solution.py:170
  (19 other events, 75.6 us)
